TPU v7x, 1024 devices: a whole 4x8x16 slice. The times are simulated.
1024 devices in a mesh: outer: 64 (over x, z_lo, core), inner: 16 (over y, z_hi).
Axes of the slice: x: 4, y: 8, z: 16 (z_hi: 2, z_lo: 8; z = z_hi * 8 + z_lo), core: 2. Of those that a mesh axis runs over, the one named last changes fastest.
Arguments:
- grads: float32 [64, 16, 524288], P('outer', 'inner'), may hold values from -0.25 to 0.25
- master: float32 [524288], P('inner'), may hold values from -3 to 3
- first_moment: float32 [524288], P('inner'), may hold values from -3 to 3
- second_moment: float32 [524288], P('inner'), may hold values from 0.05 to 1
- ranks: int32 [64], replicated, may hold values from 0 to 63, each once
Outputs:
- new_master: float32 [524288], P('inner')
- new_first: float32 [524288], P('inner')
- new_second: float32 [524288], P('inner')
- weights: bfloat16 [524288], replicated
Inputs may be any that keep to these rules, and one draw needn't show every extreme that they name: ranks is a permutation of the replica group indices.
All inputs are finite; a program needn't handle non-finite values.
Results may differ from a plain program's by a relative error of at most 0.006.
Values may be sent and summed in bfloat16 or wider, within the bound.
No kernel may reach another device: no remote copies, remote signals or barrier semaphores. Data moves between devices by JAX's collectives and lax.ppermute only.
A program may use at most 32 MiB of HBM per device.

v0:
```python
import jax
import jax.numpy as jnp
from jax import lax
from jax.sharding import PartitionSpec as P

STEP = 1000


def adamw_update(grad, master, first_moment, second_moment):
    new_first = 0.9 * first_moment + 0.1 * grad
    new_second = 0.95 * second_moment + 0.05 * grad * grad
    corr_first = 1.0 - 0.9**STEP
    corr_second = 1.0 - 0.95**STEP
    direction = new_first / corr_first / (jnp.sqrt(new_second / corr_second) + 1e-05)
    new_master = master - 0.05 * (direction + 0.1 * master)
    return (new_master, new_first, new_second)


def shards(grads, master, first_moment, second_moment, ranks):
    group_index = lax.axis_index("outer")
    group_count = lax.axis_size("outer")
    replica_rank = ranks[group_index]
    shard_weight = 1.0 + 2.0 * replica_rank.astype(jnp.float32) / (group_count - 1)
    scaled = grads[0, 0] * shard_weight
    summed = lax.psum_scatter(
        scaled.astype(jnp.bfloat16), "inner", scatter_dimension=0, tiled=True
    ).astype(jnp.float32)
    reduced = lax.psum(summed, "outer")
    new_master, new_first, new_second = adamw_update(reduced, master, first_moment, second_moment)
    weights = lax.all_gather(new_master.astype(jnp.bfloat16), "inner", axis=0, tiled=True)
    return (new_master, new_first, new_second, weights)


def solution(mesh):
    return jax.shard_map(
        shards,
        mesh=mesh,
        in_specs=(P("outer", "inner", None), P("inner"), P("inner"), P("inner"), P()),
        out_specs=(P("inner"), P("inner"), P("inner"), P()),
        check_vma=False,
    )
```

profile of v0, /device:TPU:2, one launch (start us, length us, event | category | flops | bytes accessed | tf_op | source)
XLA Modules:
  0.0 1323.7 jit_solution(11369314389858222833)
XLA Ops:
  7.2 0.0 all-reduce.6.cloned.1.call-start
  7.2 1.2 dynamic_slice.3
  9.1 0.0 copy-start
  9.1 0.0 copy-start.1
  9.1 0.0 copy-start.2
  9.1 23.8 %convert_reduce_fusion = bf16[524288]{0:T(1024)(128)(2,1)} fusion(f32[1,1,524288]{2,1,0:T(1,128)} %param.5, f32[]{:T(128)} %bitcast), kind=kLoop, calls=%fused_computation | loop fusion | flops 1048576 | bytes 3145732 | tf_op jit(solution)/shard_map/convert_element_type | solution.py:26
  32.9 0.0 all-reduce.6.cloned.1.call-update
  33.0 0.0 all-reduce.4.cloned.1.call-start
  33.0 1.3 dynamic-slice
  34.9 383.0 %all-reduce.6.cloned.1.call-done = bf16[524288]{0:T(1024)(128)(2,1)} async-done(((bf16[524288]{0:T(1024)(128)(2,1)}), bf16[524288]{0:T(1024)(128)(2,1)}) %all-reduce.6.cloned.1.call-update) | async-done | bytes 1048592
  417.9 1.5 dynamic-slice_convert_fusion
  419.4 0.0 all-reduce.4.cloned.1.call-update
  419.4 0.0 all-gather.2.cloned.1.call-start
  419.5 736.5 %all-reduce.4.cloned.1.call-done = f32[32768]{0:T(1024)} async-done(((f32[32768]{0:T(1024)}), f32[32768]{0:T(1024)}) %all-reduce.4.cloned.1.call-update) | async-done | bytes 131088 | tf_op jit(solution)/shard_map/psum | solution.py:28
  1156.0 0.0 copy-done
  1156.0 0.0 copy-done.1
  1156.0 0.0 copy-done.2
  1156.0 1.7 fusion.1
  1157.7 0.0 all-gather.2.cloned.1.call-update
  1157.7 157.1 %all-gather.2.cloned.1.call-done = bf16[524288]{0:T(1024)(128)(2,1)} async-done(((bf16[32768]{0:T(1024)(128)(2,1)}), bf16[524288]{0:T(1024)(128)(2,1)}) %all-gather.2.cloned.1.call-update) | async-done | bytes 1048592 | tf_op jit(solution)/shard_map/all_gather | solution.py:30
  1314.9 2.3 copy.12
Async XLA Ops:
  7.2 410.8 %all-reduce.6.cloned.1.call-start = ((), (), s32[]{:S(2)}) async-start(), calls=%async_computation.2 | async-start | bytes 2097152
  9.1 1146.9 %copy-start = (f32[32768]{0:T(1024)S(1)}, f32[32768]{0:T(1024)}, u32[]{:S(2)}) copy-start(f32[32768]{0:T(1024)} %param.6) | copy-start | bytes 393220
  9.1 1146.9 %copy-start.1 = (f32[32768]{0:T(1024)S(1)}, f32[32768]{0:T(1024)}, u32[]{:S(2)}) copy-start(f32[32768]{0:T(1024)} %param.8) | copy-start | bytes 393220
  9.1 1146.9 %copy-start.2 = (f32[32768]{0:T(1024)S(1)}, f32[32768]{0:T(1024)}, u32[]{:S(2)}) copy-start(f32[32768]{0:T(1024)} %param.7) | copy-start | bytes 393220
  33.0 1123.0 %all-reduce.4.cloned.1.call-start = ((), (), s32[]{:S(2)}) async-start(), calls=%async_computation | async-start | bytes 262144 | tf_op jit(solution)/shard_map/psum | solution.py:28
  419.4 895.4 %all-gather.2.cloned.1.call-start = ((), (), s32[]{:S(2)}) async-start(), calls=%async_computation.1 | async-start | bytes 1114112 | tf_op jit(solution)/shard_map/all_gather | solution.py:30
Sparse Core Ops, SparseCore 0:
  33.1 384.7 all-reduce.5
  422.0 733.9 all-reduce.3
  1161.0 153.8 all-gather.1
where the time goes:
time: 1320 us
  waiting for transfers between devices  1280 us (97%)
  other arithmetic  27 us (2%)
  between operations  15.1 us (1%)
    psum x1, waiting for transfers between devices, shards(): reduced = lax.psum(summed, 'outer')  737 us
    unnamed x4, waiting for transfers between devices  383 us
    all_gather x1, waiting for transfers between devices, shards(): lax.all_gather(new_master.astype(jnp.bfloat16), 'inner', axis=0, tiled=True)  157 us
  transfers between devices with their start and end apart: 3, of which 3 were waited for; matrix products, arithmetic and copies ran while one was open for 0% of the time, Pallas kernels for 0%

commit v1 on v0

v1 whole, which is shorter than its diff:
```python
import jax
import jax.numpy as jnp
from jax import lax
from jax.experimental import pallas as pl
from jax.experimental.pallas import tpu as pltpu
from jax.sharding import Mesh, PartitionSpec as P

STEP = 1000
bf16, f32 = jnp.bfloat16, jnp.float32
VMEM = pl.BlockSpec(memory_space=pltpu.VMEM)
SMEM = pl.BlockSpec(memory_space=pltpu.SMEM)
HBM = pl.BlockSpec(memory_space=pltpu.HBM)
SCALE_VMEM = 60 << 20
PARAMS = pltpu.CompilerParams(vmem_limit_bytes=8 << 20)

NX, NY, NC, NZL, NZH = 4, 8, 2, 8, 2
NZ = NZL * NZH
ROWS = 64
SUB = ROWS // NZL
STATE = 4 * SUB


def adamw_update(grad, master, first_moment, second_moment):
    new_first = 0.9 * first_moment + 0.1 * grad
    new_second = 0.95 * second_moment + 0.05 * grad * grad
    corr_first = 1.0 - 0.9**STEP
    corr_second = 1.0 - 0.95**STEP
    direction = new_first / corr_first / (jnp.sqrt(new_second / corr_second) + 1e-05)
    new_master = master - 0.05 * (direction + 0.1 * master)
    return (new_master, new_first, new_second)


def scale_kernel(ranks, grads, master, first, second, own, send, state, buf, sbuf, sem, ssem):
    x, zl, c = lax.axis_index("x"), lax.axis_index("zl"), lax.axis_index("c")
    halves = (1 - c, c)
    copies = [
        [pltpu.make_async_copy(grads.at[y, halves[h]], buf.at[h, y], sem.at[h, y]) for y in range(NY)]
        for h in range(2)
    ]
    at = pl.ds(pl.multiple_of(x * ROWS + zl * SUB, SUB), SUB)
    state_copies = [
        pltpu.make_async_copy(ref.at[at], sbuf.at[i], ssem.at[i])
        for i, ref in enumerate((master, first, second))
    ]
    for h in range(2):
        for copy in copies[h]:
            copy.start()
    for copy in state_copies:
        copy.start()
    outer = (x * NZL + zl) * NC + c
    weight = 1.0 + ranks[outer].astype(f32) * (2.0 / 63.0)
    for h, out in enumerate((send, own)):
        for y in range(NY):
            copies[h][y].wait()
            for k in range(NX):
                out[k, y] = (buf[h, y, pl.ds(k * ROWS, ROWS)] * weight).astype(bf16)
    for copy in state_copies:
        copy.wait()
    high = sbuf[0].astype(bf16)
    low = (sbuf[0] - high.astype(f32)).astype(bf16)
    for i, part in enumerate((high, low, sbuf[1].astype(bf16), sbuf[2].astype(bf16))):
        state[pl.ds(i * SUB, SUB)] = part


def spread_kernel(parts, state, out):
    total = parts[0].astype(f32)
    for y in range(1, NY):
        total += parts[y].astype(f32)
    total = total.astype(bf16)
    for z in range(NZ):
        out[z, pl.ds(0, ROWS)] = total
        out[z, pl.ds(ROWS, STATE)] = state[...]


def update_kernel(parts, weights, grad):
    c = lax.axis_index("c")
    total = parts[0, pl.ds(0, ROWS)].astype(f32)
    for z in range(1, NZ):
        total += parts[z, pl.ds(0, ROWS)].astype(f32)
    grad[...] = total.astype(bf16)
    for j in range(NZL):
        high, low, first, second = (
            parts[NZH * j + c, pl.ds(ROWS + i * SUB, SUB)].astype(f32) for i in range(4)
        )
        piece = adamw_update(total[j * SUB : (j + 1) * SUB], high + low, first, second)[0].astype(bf16)
        for y in range(NY):
            weights[y, pl.ds(j * SUB, SUB)] = piece


def fan_kernel(weights, grad, out):
    for x in range(NX):
        out[x, pl.ds(0, NY)] = weights[...]
        out[x, NY] = grad[...]


def finish_kernel(own, other, master, first, second, weights, new_master, new_first, new_second, sem):
    c, zh = lax.axis_index("c"), lax.axis_index("zh")
    copies = []
    for h, (ref, half) in enumerate(((own, c), (other, 1 - c))):
        for x in range(NX):
            copies.append(
                pltpu.make_async_copy(ref.at[x, pl.ds(0, NY)], weights.at[:, half, x], sem.at[h, x])
            )
    for copy in copies:
        copy.start()
    for x in range(NX):
        at = pl.ds(x * ROWS, ROWS)
        grad = jnp.where(c == zh, own[x, NY].astype(f32), other[x, NY].astype(f32))
        new_master[at], new_first[at], new_second[at] = adamw_update(grad, master[at], first[at], second[at])
    for copy in copies:
        copy.wait()


def shards(grads, master, first_moment, second_moment, ranks):
    shard = (NX * ROWS, 128)
    master, first, second = (a.reshape(shard) for a in (master, first_moment, second_moment))
    half = jax.ShapeDtypeStruct((NX, NY, ROWS, 128), bf16)
    own, send, state = pl.pallas_call(
        scale_kernel,
        out_shape=(half, half, jax.ShapeDtypeStruct((STATE, 128), bf16)),
        in_specs=[SMEM, HBM, HBM, HBM, HBM],
        out_specs=(VMEM, VMEM, VMEM),
        scratch_shapes=[
            pltpu.VMEM((2, NY) + shard, f32),
            pltpu.VMEM((3, SUB, 128), f32),
            pltpu.SemaphoreType.DMA((2, NY)),
            pltpu.SemaphoreType.DMA((3,)),
        ],
        compiler_params=pltpu.CompilerParams(vmem_limit_bytes=SCALE_VMEM),
        name="scale",
    )(ranks, grads.reshape((NY, NC) + shard), master, first, second)
    swap = [(0, 1), (1, 0)]
    got = lax.ppermute(send, "c", swap)
    half_sum = (own.astype(f32) + got.astype(f32)).astype(bf16)
    parts = lax.all_to_all(half_sum, "x", 0, 0, tiled=True)
    parts = jnp.sum(parts.astype(f32), axis=0).astype(bf16)
    parts = lax.all_to_all(parts, "y", 0, 0, tiled=True)
    parts = pl.pallas_call(
        spread_kernel,
        out_shape=jax.ShapeDtypeStruct((NZ, ROWS + STATE, 128), bf16),
        in_specs=[VMEM, VMEM],
        out_specs=VMEM,
        compiler_params=PARAMS,
        name="spread",
    )(parts, state)
    parts = lax.all_to_all(parts, ("zl", "zh"), 0, 0, tiled=True)
    weights, grad = pl.pallas_call(
        update_kernel,
        out_shape=(
            jax.ShapeDtypeStruct((NY, ROWS, 128), bf16),
            jax.ShapeDtypeStruct((ROWS, 128), bf16),
        ),
        in_specs=[VMEM],
        out_specs=(VMEM, VMEM),
        compiler_params=PARAMS,
        name="update",
    )(parts)
    weights = lax.all_to_all(weights, "y", 0, 0, tiled=True)
    fan = pl.pallas_call(
        fan_kernel,
        out_shape=jax.ShapeDtypeStruct((NX, NY + 1, ROWS, 128), bf16),
        in_specs=[VMEM, VMEM],
        out_specs=VMEM,
        compiler_params=PARAMS,
        name="fan",
    )(weights, grad)
    fan = lax.all_to_all(fan, "x", 0, 0, tiled=True)
    other = lax.ppermute(fan, "c", swap)
    out = jax.ShapeDtypeStruct(shard, f32)
    weights, new_master, new_first, new_second = pl.pallas_call(
        finish_kernel,
        out_shape=(jax.ShapeDtypeStruct((NY, NC, NX, ROWS, 128), bf16), out, out, out),
        in_specs=[VMEM] * 5,
        out_specs=(HBM, VMEM, VMEM, VMEM),
        scratch_shapes=[pltpu.SemaphoreType.DMA((2, NX))],
        compiler_params=PARAMS,
        name="finish",
    )(fan, other, master, first, second)
    return (new_master.reshape(-1), new_first.reshape(-1), new_second.reshape(-1), weights.reshape(-1))


def solution(mesh):
    fine = Mesh(mesh.devices.reshape(NX, NZL, NC, NY, NZH), ("x", "zl", "c", "y", "zh"))
    shard = P(("y", "zh"))
    return jax.shard_map(
        shards,
        mesh=fine,
        in_specs=(P(("x", "zl", "c"), ("y", "zh"), None), shard, shard, shard, P()),
        out_specs=(shard, shard, shard, P()),
        check_vma=False,
    )
```

time: 1320 us -> 111 us (0.08)
  the two profiles are of different devices: /device:TPU:2 before, /device:TPU:65 now
where the time goes in v1:
time: 111 us; the launch traced here: 110 us
  blocking collectives  81.9 us (74%)
  starting transfers between devices  17.5 us (16%)
  Pallas kernels  5.4 us (5%)
  waiting for transfers between devices  3.33 us (3%)
  other arithmetic  1.3 us (1%)
    all_to_all x1, blocking collectives, shards(): parts = lax.all_to_all(parts, ('zl', 'zh'), 0, 0, tiled=True)  34.7 us
    ppermute x1, starting transfers between devices, shards(): other = lax.ppermute(fan, 'c', swap)  14.9 us
    all_to_all x1, blocking collectives, shards(): parts = lax.all_to_all(parts, 'y', 0, 0, tiled=True)  14.8 us
    all_to_all x1, blocking collectives, shards(): parts = lax.all_to_all(half_sum, 'x', 0, 0, tiled=True)  12.4 us
    all_to_all x1, blocking collectives, shards(): weights = lax.all_to_all(weights, 'y', 0, 0, tiled=True)  10.3 us
    all_to_all x1, blocking collectives, shards(): fan = lax.all_to_all(fan, 'x', 0, 0, tiled=True)  9.67 us
    pallas_call x1, Pallas kernels, shards(): pl.pallas_call(scale_kernel, out_shape=(half, half, jax.ShapeDtypeStruct(...  3.43 us
    ppermute x1, starting transfers between devices, shards(): got = lax.ppermute(send, 'c', swap)  2.58 us
  transfers between devices with their start and end apart: 2, of which 2 were waited for; matrix products, arithmetic and copies ran while one was open for 0% of the time, Pallas kernels for 0%

profile of v1, /device:TPU:65, one launch (start us, length us, event | category | flops | bytes accessed | tf_op | source)
XLA Modules:
  0.0 110.1 jit_solution(5282163403407001571)
XLA Ops:
  0.6 3.4 %scale.1 = (bf16[4,8,64,128]{3,2,1,0:T(8,128)(2,1)}, bf16[4,8,64,128]{3,2,1,0:T(8,128)(2,1)}, bf16[32,128]{1,0:T(8,128)(2,1)}) custom-call(s32[64]{0:T(128)} %ranks.1, f32[8,2,256,128]{3,2,1,0:T(8,128)} %bitcast.14, f32[256,128]{1,0:T(8,128)} %bitcast.8, f32[256,128]{1,0:T(8,128)} %bitcast.10, f32[256,128]{1,0:T(8,128)} %bitcast.12), custom_call_target="tpu_custom_call" | custom-call | tf_op jit(solution)/shard_map/scale/pallas_call | solution.py:118
  4.1 0.0 copy-start.3
  4.1 2.6 %collective-permute-start = (bf16[4,8,64,128]{3,2,1,0:T(8,128)(2,1)}, bf16[4,8,64,128]{3,2,1,0:T(8,128)(2,1)S(1)}, u32[]{:S(2)}, u32[]{:S(2)}) collective-permute-start(bf16[4,8,64,128]{3,2,1,0:T(8,128)(2,1)} %get-tuple-element.14), channel_id=1, source_target_pairs={{0,16},{16,0},{1,17},{17,1},{2,18},{18,2},{3,19},{19,3},{4,20},{20... | collective-permute-start | bytes 1572872 | tf_op jit(solution)/shard_map/ppermute | solution.py:133
  6.7 1.7 %collective-permute-done = bf16[4,8,64,128]{3,2,1,0:T(8,128)(2,1)S(1)} collective-permute-done((bf16[4,8,64,128]{3,2,1,0:T(8,128)(2,1)}, bf16[4,8,64,128]{3,2,1,0:T(8,128)(2,1)S(1)}, u32[]{:S(2)}, u32[]{:S(2)}) %collective-permute-start) | collective-permute-done | bytes 524320 | tf_op jit(solution)/shard_map/ppermute | solution.py:133
  8.4 1.2 %add_convert_fusion = bf16[4,8,64,128]{3,2,1,0:T(8,128)(2,1)S(1)} fusion(bf16[4,8,64,128]{3,2,1,0:T(8,128)(2,1)S(1)} %collective-permute-done, bf16[4,8,64,128]{3,2,1,0:T(8,128)(2,1)} %get-tuple-element.13), kind=kLoop, calls=%fused_computation | loop fusion | flops 1048576 | bytes 1572864 | tf_op jit(solution)/shard_map/convert_element_type | solution.py:134
  9.6 12.4 %all_to_all.25 = bf16[4,8,64,128]{3,2,1,0:T(8,128)(2,1)S(1)} all-to-all(bf16[4,8,64,128]{3,2,1,0:T(8,128)(2,1)S(1)} %add_convert_fusion), channel_id=1, replica_groups=mesh['x'=4,'zl'=8,'c'=2,'y'=8,'zh'=2] {'x'}, dimensions={0} | all-to-all | bytes 1048576 | tf_op jit(solution)/shard_map/all_to_all | solution.py:135
  22.1 0.1 reduce_sum.12
  22.2 0.0 copy-start
  22.2 0.0 copy-start.1
  22.2 0.0 copy-start.2
  22.2 14.8 %all_to_all.26.parts = bf16[8,64,128]{2,1,0:T(8,128)(2,1)S(1)} all-to-all(bf16[8,64,128]{2,1,0:T(8,128)(2,1)S(1)} %reduce_sum.12), channel_id=1, replica_groups=mesh['x'=4,'zl'=8,'c'=2,'y'=8,'zh'=2] {'y'}, dimensions={0} | all-to-all | bytes 262144 | tf_op jit(solution)/shard_map/all_to_all | solution.py:137
  37.0 0.0 copy-done.3
  37.0 34.7 %all_to_all.27.parts = bf16[16,96,128]{2,1,0:T(8,128)(2,1)S(1)} all-to-all(bf16[16,96,128]{2,1,0:T(8,128)(2,1)S(1)} %spread.1), channel_id=1, replica_groups=mesh['x'=4,'zl'=8,'c'=2,'y'=8,'zh'=2] {'zl','zh'}, dimensions={0} | all-to-all | bytes 786432 | tf_op jit(solution)/shard_map/all_to_all | solution.py:146
  71.7 0.1 update.1
  71.8 10.3 %all_to_all.28.weights = bf16[8,64,128]{2,1,0:T(8,128)(2,1)S(1)} all-to-all(bf16[8,64,128]{2,1,0:T(8,128)(2,1)S(1)} %get-tuple-element.16), channel_id=1, replica_groups=mesh['x'=4,'zl'=8,'c'=2,'y'=8,'zh'=2] {'y'}, dimensions={0} | all-to-all | bytes 262144 | tf_op jit(solution)/shard_map/all_to_all | solution.py:158
  82.1 0.1 fan.1
  82.2 9.7 %all_to_all.29.own = bf16[4,9,64,128]{3,2,1,0:T(8,128)(2,1)S(1)} all-to-all(bf16[4,9,64,128]{3,2,1,0:T(8,128)(2,1)S(1)} %fan.1), channel_id=1, replica_groups=mesh['x'=4,'zl'=8,'c'=2,'y'=8,'zh'=2] {'x'}, dimensions={0} | all-to-all | bytes 1179648 | tf_op jit(solution)/shard_map/all_to_all | solution.py:167
  91.8 14.9 %collective-permute-start.1 = (bf16[4,9,64,128]{3,2,1,0:T(8,128)(2,1)S(1)}, bf16[4,9,64,128]{3,2,1,0:T(8,128)(2,1)S(1)}, u32[]{:S(2)}, u32[]{:S(2)}) collective-permute-start(bf16[4,9,64,128]{3,2,1,0:T(8,128)(2,1)S(1)} %all_to_all.29.own), channel_id=1, source_target_pairs={{0,16},{16,0},{1,17},{17,1},{2,18},{18,2},{3,19},{19,3},{4,20},{20... | collective-permute-start | bytes 1769480 | tf_op jit(solution)/shard_map/ppermute | solution.py:168
  106.7 1.6 %collective-permute-done.1.other = bf16[4,9,64,128]{3,2,1,0:T(8,128)(2,1)S(1)} collective-permute-done((bf16[4,9,64,128]{3,2,1,0:T(8,128)(2,1)S(1)}, bf16[4,9,64,128]{3,2,1,0:T(8,128)(2,1)S(1)}, u32[]{:S(2)}, u32[]{:S(2)}) %collective-permute-start.1) | collective-permute-done | bytes 589856 | tf_op jit(solution)/shard_map/ppermute | solution.py:168
  108.3 0.0 copy-done
  108.3 0.0 copy-done.1
  108.3 0.0 copy-done.2
  108.3 1.8 %finish.1 = (bf16[8,2,4,64,128]{4,3,2,1,0:T(8,128)(2,1)}, f32[256,128]{1,0:T(8,128)}, f32[256,128]{1,0:T(8,128)}, f32[256,128]{1,0:T(8,128)}) custom-call(bf16[4,9,64,128]{3,2,1,0:T(8,128)(2,1)S(1)} %all_to_all.29.own, bf16[4,9,64,128]{3,2,1,0:T(8,128)(2,1)S(1)} %collective-permute-done.1.other, f32[256,128]{1,0:T(8,128)S(1)} %bitcast.9, ...), custom_call_target="tpu_custom_call" | custom-call | tf_op jit(solution)/shard_map/finish/pallas_call | solution.py:170
  (1 shorter events, 0.0 us)
Async XLA Ops:
  4.1 32.9 %copy-start.3 = (bf16[32,128]{1,0:T(8,128)(2,1)S(1)}, bf16[32,128]{1,0:T(8,128)(2,1)}, u32[]{:S(2)}) copy-start(bf16[32,128]{1,0:T(8,128)(2,1)} %get-tuple-element.15.state) | copy-start | bytes 24580
  4.1 4.3 %collective-permute-start = (bf16[4,8,64,128]{3,2,1,0:T(8,128)(2,1)}, bf16[4,8,64,128]{3,2,1,0:T(8,128)(2,1)S(1)}, u32[]{:S(2)}, u32[]{:S(2)}) collective-permute-start(bf16[4,8,64,128]{3,2,1,0:T(8,128)(2,1)} %get-tuple-element.14), channel_id=1, source_target_pairs={{0,16},{16,0},{1,17},{17,1},{2,18},{18,2},{3,19},{19,3},{4,20},{20... | collective-permute-start | bytes 1572872 | tf_op jit(solution)/shard_map/ppermute | solution.py:133
  22.2 86.2 %copy-start = (f32[32768]{0:T(1024)S(1)}, f32[32768]{0:T(1024)}, u32[]{:S(2)}) copy-start(f32[32768]{0:T(1024)} %param.6) | copy-start | bytes 393220
  22.2 86.2 %copy-start.1 = (f32[32768]{0:T(1024)S(1)}, f32[32768]{0:T(1024)}, u32[]{:S(2)}) copy-start(f32[32768]{0:T(1024)} %param.7) | copy-start | bytes 393220
  22.2 86.2 %copy-start.2 = (f32[32768]{0:T(1024)S(1)}, f32[32768]{0:T(1024)}, u32[]{:S(2)}) copy-start(f32[32768]{0:T(1024)} %param.8) | copy-start | bytes 393220
  91.8 16.5 %collective-permute-start.1 = (bf16[4,9,64,128]{3,2,1,0:T(8,128)(2,1)S(1)}, bf16[4,9,64,128]{3,2,1,0:T(8,128)(2,1)S(1)}, u32[]{:S(2)}, u32[]{:S(2)}) collective-permute-start(bf16[4,9,64,128]{3,2,1,0:T(8,128)(2,1)S(1)} %all_to_all.29.own), channel_id=1, source_target_pairs={{0,16},{16,0},{1,17},{17,1},{2,18},{18,2},{3,19},{19,3},{4,20},{20... | collective-permute-start | bytes 1769480 | tf_op jit(solution)/shard_map/ppermute | solution.py:168

commit v2 on v0

v2 whole, which is shorter than its diff:
```python
import functools

import jax
import jax.numpy as jnp
from jax import lax
from jax.experimental import pallas as pl
from jax.experimental.pallas import tpu as pltpu
from jax.sharding import Mesh, PartitionSpec as P

STEP = 1000
bf16, f32 = jnp.bfloat16, jnp.float32
VMEM = pl.BlockSpec(memory_space=pltpu.VMEM)
HBM = pl.BlockSpec(memory_space=pltpu.HBM)
SCALE_VMEM = 60 << 20
PARAMS = pltpu.CompilerParams(vmem_limit_bytes=8 << 20)

NX, NY, NC, NZL, NZH = 4, 8, 2, 8, 2
NZ = NZL * NZH
NS = NY * NZH
ROWS = 32


def adamw_update(grad, master, first_moment, second_moment):
    new_first = 0.9 * first_moment + 0.1 * grad
    new_second = 0.95 * second_moment + 0.05 * grad * grad
    corr_first = 1.0 - 0.9**STEP
    corr_second = 1.0 - 0.95**STEP
    direction = new_first / corr_first / (jnp.sqrt(new_second / corr_second) + 1e-05)
    new_master = master - 0.05 * (direction + 0.1 * master)
    return (new_master, new_first, new_second)


def scale_kernel(core, ranks, grads, out, buf, rank, sem, rank_sem):
    x, zl, c = lax.axis_index("x"), lax.axis_index("zl"), lax.axis_index("c")
    half = 1 - c if core else c
    copies = [pltpu.make_async_copy(grads.at[y, :, half], buf.at[y], sem.at[y]) for y in range(NY)]
    rank_copy = pltpu.make_async_copy(ranks, rank, rank_sem)
    rank_copy.start()
    for copy in copies:
        copy.start()
    rank_copy.wait()
    outer = (x * NZL + zl) * NC + c
    weight = 1.0 + rank[outer].astype(f32) * (2.0 / 63.0)
    for y in range(NY):
        copies[y].wait()
        for k in range(NX):
            for z in range(NZH):
                out[k, y, z] = (buf[y, z, pl.ds(k * ROWS, ROWS)] * weight).astype(bf16)


def spread_kernel(parts, out):
    total = parts[0].astype(f32)
    for y in range(1, NY):
        total += parts[y].astype(f32)
    total = total.astype(bf16)
    for z in range(NZL):
        for zh in range(NZH):
            out[z * NZH + zh] = total[zh]


def update_kernel(parts, master, first, second, weights, grad):
    at = pl.ds(pl.multiple_of((lax.axis_index("c") * NX + lax.axis_index("x")) * ROWS, ROWS), ROWS)
    total = parts[0].astype(f32)
    for z in range(1, NZ):
        total += parts[z].astype(f32)
    total = total.astype(bf16)
    grad[...] = total
    piece = adamw_update(total.astype(f32), master[at], first[at], second[at])[0].astype(bf16)
    for s in range(NS):
        weights[s] = piece


def fan_kernel(weights, grad, out):
    for x in range(NX):
        out[x, pl.ds(0, NS)] = weights[...]
        out[x, NS] = grad[...]


def finish_kernel(own, other, master, first, second, weights, new_master, new_first, new_second, sem):
    c = lax.axis_index("c")
    sides = ((own, c), (other, 1 - c))
    copies = [
        pltpu.make_async_copy(ref.at[x, pl.ds(0, NS)], weights.at[:, half, x], sem.at[h, x])
        for h, (ref, half) in enumerate(sides)
        for x in range(NX)
    ]
    for copy in copies:
        copy.start()
    for ref, half in sides:
        for x in range(NX):
            at = pl.ds(pl.multiple_of((half * NX + x) * ROWS, ROWS), ROWS)
            new_master[at], new_first[at], new_second[at] = adamw_update(
                ref[x, NS].astype(f32), master[at], first[at], second[at]
            )
    for copy in copies:
        copy.wait()


def shards(grads, master, first_moment, second_moment, ranks):
    shard = (NC * NX * ROWS, 128)
    master, first, second = (a.reshape(shard) for a in (master, first_moment, second_moment))
    grads = grads.reshape((NY, NZH, NC, NX * ROWS, 128))

    def scaled(core):
        return pl.pallas_call(
            functools.partial(scale_kernel, core),
            out_shape=jax.ShapeDtypeStruct((NX, NY, NZH, ROWS, 128), bf16),
            in_specs=[HBM, HBM],
            out_specs=VMEM,
            scratch_shapes=[
                pltpu.VMEM((NY, NZH, NX * ROWS, 128), f32),
                pltpu.SMEM((64,), jnp.int32),
                pltpu.SemaphoreType.DMA((NY,)),
                pltpu.SemaphoreType.DMA,
            ],
            compiler_params=pltpu.CompilerParams(vmem_limit_bytes=SCALE_VMEM),
            cost_estimate=pl.CostEstimate(flops=1 << 18, bytes_accessed=3 << 19, transcendentals=0),
            name="scale_send" if core else "scale_own",
        )(ranks, grads)

    def local(kernel, out_shape, *operands):
        return pl.pallas_call(
            kernel,
            out_shape=out_shape,
            in_specs=[VMEM] * len(operands),
            out_specs=jax.tree.map(lambda _: VMEM, out_shape),
            compiler_params=PARAMS,
            name=kernel.__name__,
        )(*operands)

    swap = [(0, 1), (1, 0)]
    got = lax.ppermute(scaled(1), "c", swap)
    parts = (scaled(0).astype(f32) + got.astype(f32)).astype(bf16)
    parts = lax.all_to_all(parts, "x", 0, 0, tiled=True)
    parts = jnp.sum(parts.astype(f32), axis=0).astype(bf16)
    parts = lax.all_to_all(parts, "y", 0, 0, tiled=True)
    parts = local(spread_kernel, jax.ShapeDtypeStruct((NZ, ROWS, 128), bf16), parts)
    parts = lax.all_to_all(parts, ("zl", "zh"), 0, 0, tiled=True)
    piece = jax.ShapeDtypeStruct((ROWS, 128), bf16)
    weights, grad = local(
        update_kernel, (jax.ShapeDtypeStruct((NS, ROWS, 128), bf16), piece), parts, master, first, second
    )
    mirrors = [
        [(z % NZL) * NS + y * NZH + z // NZL for y in range(NY) for z in (low, NZ - 1 - low)]
        for low in range(NZL)
    ]
    weights = lax.all_to_all(weights, ("zl", "y", "zh"), 0, 0, tiled=True, axis_index_groups=mirrors)
    fan = local(fan_kernel, jax.ShapeDtypeStruct((NX, NS + 1, ROWS, 128), bf16), weights, grad)
    fan = lax.all_to_all(fan, "x", 0, 0, tiled=True)
    other = lax.ppermute(fan, "c", swap)
    out = jax.ShapeDtypeStruct(shard, f32)
    weights, new_master, new_first, new_second = pl.pallas_call(
        finish_kernel,
        out_shape=(jax.ShapeDtypeStruct((NS, NC, NX, ROWS, 128), bf16), out, out, out),
        in_specs=[VMEM] * 5,
        out_specs=(HBM, VMEM, VMEM, VMEM),
        scratch_shapes=[pltpu.SemaphoreType.DMA((2, NX))],
        compiler_params=PARAMS,
        name="finish",
    )(fan, other, master, first, second)
    return (new_master.reshape(-1), new_first.reshape(-1), new_second.reshape(-1), weights.reshape(-1))


def solution(mesh):
    fine = Mesh(mesh.devices.reshape(NX, NZL, NC, NY, NZH), ("x", "zl", "c", "y", "zh"))
    shard = P(("y", "zh"))
    return jax.shard_map(
        shards,
        mesh=fine,
        in_specs=(P(("x", "zl", "c"), ("y", "zh"), None), shard, shard, shard, P()),
        out_specs=(shard, shard, shard, P()),
        check_vma=False,
    )
```

time: 1320 us -> 104 us (0.08)
  the two profiles are of different devices: /device:TPU:2 before, /device:TPU:193 now
where the time goes in v2:
time: 104 us
  blocking collectives  83.1 us (80%)
  starting transfers between devices  10.7 us (10%)
  Pallas kernels  6.28 us (6%)
  waiting for transfers between devices  1.56 us (2%)
  other arithmetic  1.37 us (1%)
    all_to_all x1, blocking collectives, shards(): parts = lax.all_to_all(parts, ('zl', 'zh'), 0, 0, tiled=True)  26.8 us
    all_to_all x1, blocking collectives, shards(): lax.all_to_all(weights, ('zl', 'y', 'zh'), 0, 0, tiled=True, axis_index_g...  19 us
    all_to_all x1, blocking collectives, shards(): parts = lax.all_to_all(parts, 'y', 0, 0, tiled=True)  14.6 us
    all_to_all x1, blocking collectives, shards(): parts = lax.all_to_all(parts, 'x', 0, 0, tiled=True)  13.1 us
    all_to_all x1, blocking collectives, shards(): fan = lax.all_to_all(fan, 'x', 0, 0, tiled=True)  9.48 us
    ppermute x1, starting transfers between devices, shards(): other = lax.ppermute(fan, 'c', swap)  8.09 us
    pallas_call x2, Pallas kernels, scaled(): pl.pallas_call(functools.partial(scale_kernel, core), out_shape=jax.Shape...  4.35 us
    ppermute x1, starting transfers between devices, shards(): got = lax.ppermute(scaled(1), 'c', swap)  2.58 us
  transfers between devices with their start and end apart: 2, of which 1 were waited for; matrix products, arithmetic and copies ran while one was open for 0% of the time, Pallas kernels for 2%

profile of v2, /device:TPU:193, one launch (start us, length us, event | category | flops | bytes accessed | tf_op | source)
XLA Modules:
  0.0 103.7 jit_solution(13563849215370737188)
XLA Ops:
  0.6 2.2 %scale_send.1 = bf16[4,8,2,32,128]{4,3,2,1,0:T(8,128)(2,1)} custom-call(s32[64]{0:T(128)} %ranks.3, f32[8,2,2,128,128]{4,3,2,1,0:T(8,128)} %bitcast.14), custom_call_target="tpu_custom_call" | custom-call | flops 262144 | bytes 1572864 | tf_op jit(solution)/shard_map/scale_send/pallas_call | solution.py:105
  2.8 2.6 %collective-permute-start = (bf16[4,8,2,32,128]{4,3,2,1,0:T(8,128)(2,1)}, bf16[4,8,2,32,128]{4,3,2,1,0:T(8,128)(2,1)S(1)}, u32[]{:S(2)}, u32[]{:S(2)}) collective-permute-start(bf16[4,8,2,32,128]{4,3,2,1,0:T(8,128)(2,1)} %scale_send.1), channel_id=1, source_target_pairs={{0,16},{16,0},{1,17},{17,1},{2,18},{18,2},{3,19},{19,3},{4,20},{20... | collective-permute-start | bytes 1572872 | tf_op jit(solution)/shard_map/ppermute | solution.py:132
  5.4 2.2 %scale_own.1 = bf16[4,8,2,32,128]{4,3,2,1,0:T(8,128)(2,1)} custom-call(s32[64]{0:T(128)} %ranks.3, f32[8,2,2,128,128]{4,3,2,1,0:T(8,128)} %bitcast.15), custom_call_target="tpu_custom_call" | custom-call | flops 262144 | bytes 1572864 | tf_op jit(solution)/shard_map/scale_own/pallas_call | solution.py:105
  7.6 0.0 copy-start
  7.6 0.0 copy-start.1
  7.6 0.0 copy-start.2
  7.6 0.0 collective-permute-done
  7.6 1.3 %add_convert_fusion = bf16[4,8,2,32,128]{4,3,2,1,0:T(8,128)(2,1)S(1)} fusion(bf16[4,8,2,32,128]{4,3,2,1,0:T(8,128)(2,1)S(1)} %collective-permute-done, bf16[4,8,2,32,128]{4,3,2,1,0:T(8,128)(2,1)} %scale_own.1), kind=kLoop, calls=%fused_computation | loop fusion | flops 1048576 | bytes 1572864 | tf_op jit(solution)/shard_map/convert_element_type | solution.py:133
  8.9 13.1 %all_to_all.25 = bf16[4,8,2,32,128]{4,3,2,1,0:T(8,128)(2,1)S(1)} all-to-all(bf16[4,8,2,32,128]{4,3,2,1,0:T(8,128)(2,1)S(1)} %add_convert_fusion), channel_id=1, replica_groups=mesh['x'=4,'zl'=8,'c'=2,'y'=8,'zh'=2] {'x'}, dimensions={0} | all-to-all | bytes 1048576 | tf_op jit(solution)/shard_map/all_to_all | solution.py:134
  22.0 0.1 reduce_sum.12
  22.1 14.6 %all_to_all.26.parts = bf16[8,2,32,128]{3,2,1,0:T(8,128)(2,1)S(1)} all-to-all(bf16[8,2,32,128]{3,2,1,0:T(8,128)(2,1)S(1)} %reduce_sum.12), channel_id=1, replica_groups=mesh['x'=4,'zl'=8,'c'=2,'y'=8,'zh'=2] {'y'}, dimensions={0} | all-to-all | bytes 262144 | tf_op jit(solution)/shard_map/all_to_all | solution.py:136
  36.8 26.8 %all_to_all.27.parts = bf16[16,32,128]{2,1,0:T(8,128)(2,1)S(1)} all-to-all(bf16[16,32,128]{2,1,0:T(8,128)(2,1)S(1)} %spread_kernel.1), channel_id=1, replica_groups=mesh['x'=4,'zl'=8,'c'=2,'y'=8,'zh'=2] {'zl','zh'}, dimensions={0} | all-to-all | bytes 262144 | tf_op jit(solution)/shard_map/all_to_all | solution.py:138
  63.6 0.0 copy-done
  63.6 0.0 copy-done.1
  63.6 0.0 copy-done.2
  63.6 0.1 update_kernel.1
  63.7 19.0 %all_to_all.28.weights = bf16[16,32,128]{2,1,0:T(8,128)(2,1)S(1)} all-to-all(bf16[16,32,128]{2,1,0:T(8,128)(2,1)S(1)} %get-tuple-element.10), channel_id=1, replica_groups={{0,225,2,227,4,229,6,231,8,233,10,235,12,237,14,239},{32,193,34,195,36,..., dimensions={0} | all-to-all | bytes 262144 | tf_op jit(solution)/shard_map/all_to_all | solution.py:147
  82.7 0.1 fan_kernel.1
  82.8 9.5 %all_to_all.29.own = bf16[4,17,32,128]{3,2,1,0:T(8,128)(2,1)S(1)} all-to-all(bf16[4,17,32,128]{3,2,1,0:T(8,128)(2,1)S(1)} %fan_kernel.1), channel_id=1, replica_groups=mesh['x'=4,'zl'=8,'c'=2,'y'=8,'zh'=2] {'x'}, dimensions={0} | all-to-all | bytes 1114112 | tf_op jit(solution)/shard_map/all_to_all | solution.py:149
  92.2 8.1 %collective-permute-start.1 = (bf16[4,17,32,128]{3,2,1,0:T(8,128)(2,1)S(1)}, bf16[4,17,32,128]{3,2,1,0:T(8,128)(2,1)S(1)}, u32[]{:S(2)}, u32[]{:S(2)}) collective-permute-start(bf16[4,17,32,128]{3,2,1,0:T(8,128)(2,1)S(1)} %all_to_all.29.own), channel_id=1, source_target_pairs={{0,16},{16,0},{1,17},{17,1},{2,18},{18,2},{3,19},{19,3},{4,20},{20... | collective-permute-start | bytes 1671176 | tf_op jit(solution)/shard_map/ppermute | solution.py:150
  100.3 1.6 %collective-permute-done.1.other = bf16[4,17,32,128]{3,2,1,0:T(8,128)(2,1)S(1)} collective-permute-done((bf16[4,17,32,128]{3,2,1,0:T(8,128)(2,1)S(1)}, bf16[4,17,32,128]{3,2,1,0:T(8,128)(2,1)S(1)}, u32[]{:S(2)}, u32[]{:S(2)}) %collective-permute-start.1) | collective-permute-done | bytes 557088 | tf_op jit(solution)/shard_map/ppermute | solution.py:150
  101.9 1.8 %finish.1 = (bf16[16,2,4,32,128]{4,3,2,1,0:T(8,128)(2,1)}, f32[256,128]{1,0:T(8,128)}, f32[256,128]{1,0:T(8,128)}, f32[256,128]{1,0:T(8,128)}) custom-call(bf16[4,17,32,128]{3,2,1,0:T(8,128)(2,1)S(1)} %all_to_all.29.own, bf16[4,17,32,128]{3,2,1,0:T(8,128)(2,1)S(1)} %collective-permute-done.1.other, f32[256,128]{1,0:T(8,128)S(1)} %bitcast.9, ...), custom_call_target="tpu_custom_call" | custom-call | tf_op jit(solution)/shard_map/finish/pallas_call | solution.py:152
  (1 shorter events, 0.0 us)
Async XLA Ops:
  2.8 4.8 %collective-permute-start = (bf16[4,8,2,32,128]{4,3,2,1,0:T(8,128)(2,1)}, bf16[4,8,2,32,128]{4,3,2,1,0:T(8,128)(2,1)S(1)}, u32[]{:S(2)}, u32[]{:S(2)}) collective-permute-start(bf16[4,8,2,32,128]{4,3,2,1,0:T(8,128)(2,1)} %scale_send.1), channel_id=1, source_target_pairs={{0,16},{16,0},{1,17},{17,1},{2,18},{18,2},{3,19},{19,3},{4,20},{20... | collective-permute-start | bytes 1572872 | tf_op jit(solution)/shard_map/ppermute | solution.py:132
  7.6 56.0 %copy-start = (f32[32768]{0:T(1024)S(1)}, f32[32768]{0:T(1024)}, u32[]{:S(2)}) copy-start(f32[32768]{0:T(1024)} %param.6) | copy-start | bytes 393220
  7.6 56.0 %copy-start.1 = (f32[32768]{0:T(1024)S(1)}, f32[32768]{0:T(1024)}, u32[]{:S(2)}) copy-start(f32[32768]{0:T(1024)} %param.7) | copy-start | bytes 393220
  7.6 56.0 %copy-start.2 = (f32[32768]{0:T(1024)S(1)}, f32[32768]{0:T(1024)}, u32[]{:S(2)}) copy-start(f32[32768]{0:T(1024)} %param.8) | copy-start | bytes 393220
  92.2 9.7 %collective-permute-start.1 = (bf16[4,17,32,128]{3,2,1,0:T(8,128)(2,1)S(1)}, bf16[4,17,32,128]{3,2,1,0:T(8,128)(2,1)S(1)}, u32[]{:S(2)}, u32[]{:S(2)}) collective-permute-start(bf16[4,17,32,128]{3,2,1,0:T(8,128)(2,1)S(1)} %all_to_all.29.own), channel_id=1, source_target_pairs={{0,16},{16,0},{1,17},{17,1},{2,18},{18,2},{3,19},{19,3},{4,20},{20... | collective-permute-start | bytes 1671176 | tf_op jit(solution)/shard_map/ppermute | solution.py:150

commit v3 on v2

--- a/solution.py
+++ b/solution.py
@@ -11,7 +11,6 @@
 bf16, f32 = jnp.bfloat16, jnp.float32
 VMEM = pl.BlockSpec(memory_space=pltpu.VMEM)
 HBM = pl.BlockSpec(memory_space=pltpu.HBM)
-SCALE_VMEM = 60 << 20
 PARAMS = pltpu.CompilerParams(vmem_limit_bytes=8 << 20)
 
 NX, NY, NC, NZL, NZH = 4, 8, 2, 8, 2
@@ -48,6 +47,11 @@
                 out[k, y, z] = (buf[y, z, pl.ds(k * ROWS, ROWS)] * weight).astype(bf16)
 
 
+def combine_kernel(own, got, out):
+    for x in range(NX):
+        out[x] = (own[x].astype(f32) + got[x].astype(f32)).astype(bf16)
+
+
 def spread_kernel(parts, out):
     total = parts[0].astype(f32)
     for y in range(1, NY):
@@ -76,22 +80,24 @@
         out[x, NS] = grad[...]
 
 
-def finish_kernel(own, other, master, first, second, weights, new_master, new_first, new_second, sem):
-    c = lax.axis_index("c")
-    sides = ((own, c), (other, 1 - c))
+def finish_kernel(partner, *refs):
+    ref, master, first, second, *_, weights, new_master, new_first, new_second, state, sem, state_sem = refs
+    half = lax.axis_index("c")
+    half = 1 - half if partner else half
     copies = [
-        pltpu.make_async_copy(ref.at[x, pl.ds(0, NS)], weights.at[:, half, x], sem.at[h, x])
-        for h, (ref, half) in enumerate(sides)
-        for x in range(NX)
+        pltpu.make_async_copy(ref.at[x, pl.ds(0, NS)], weights.at[:, half, x], sem.at[x]) for x in range(NX)
     ]
     for copy in copies:
         copy.start()
-    for ref, half in sides:
-        for x in range(NX):
-            at = pl.ds(pl.multiple_of((half * NX + x) * ROWS, ROWS), ROWS)
-            new_master[at], new_first[at], new_second[at] = adamw_update(
-                ref[x, NS].astype(f32), master[at], first[at], second[at]
-            )
+    rows = pl.ds(pl.multiple_of(half * NX * ROWS, ROWS), NX * ROWS)
+    for x in range(NX):
+        at = pl.ds(pl.multiple_of((half * NX + x) * ROWS, ROWS), ROWS)
+        new = adamw_update(ref[x, NS].astype(f32), master[at], first[at], second[at])
+        for i in range(3):
+            state[i, pl.ds(x * ROWS, ROWS)] = new[i]
+    for i, out in enumerate((new_master, new_first, new_second)):
+        copies.append(pltpu.make_async_copy(state.at[i], out.at[rows], state_sem.at[i]))
+        copies[-1].start()
     for copy in copies:
         copy.wait()
 
@@ -113,7 +119,7 @@
                 pltpu.SemaphoreType.DMA((NY,)),
                 pltpu.SemaphoreType.DMA,
             ],
-            compiler_params=pltpu.CompilerParams(vmem_limit_bytes=SCALE_VMEM),
+            compiler_params=pltpu.CompilerParams(vmem_limit_bytes=(60 if core else 52) << 20),
             cost_estimate=pl.CostEstimate(flops=1 << 18, bytes_accessed=3 << 19, transcendentals=0),
             name="scale_send" if core else "scale_own",
         )(ranks, grads)
@@ -130,7 +136,8 @@
 
     swap = [(0, 1), (1, 0)]
     got = lax.ppermute(scaled(1), "c", swap)
-    parts = (scaled(0).astype(f32) + got.astype(f32)).astype(bf16)
+    half = jax.ShapeDtypeStruct((NX, NY, NZH, ROWS, 128), bf16)
+    parts = local(combine_kernel, half, scaled(0), got)
     parts = lax.all_to_all(parts, "x", 0, 0, tiled=True)
     parts = jnp.sum(parts.astype(f32), axis=0).astype(bf16)
     parts = lax.all_to_all(parts, "y", 0, 0, tiled=True)
@@ -149,15 +156,24 @@
     fan = lax.all_to_all(fan, "x", 0, 0, tiled=True)
     other = lax.ppermute(fan, "c", swap)
     out = jax.ShapeDtypeStruct(shard, f32)
-    weights, new_master, new_first, new_second = pl.pallas_call(
-        finish_kernel,
-        out_shape=(jax.ShapeDtypeStruct((NS, NC, NX, ROWS, 128), bf16), out, out, out),
-        in_specs=[VMEM] * 5,
-        out_specs=(HBM, VMEM, VMEM, VMEM),
-        scratch_shapes=[pltpu.SemaphoreType.DMA((2, NX))],
-        compiler_params=PARAMS,
-        name="finish",
-    )(fan, other, master, first, second)
+    outs = ()
+    for partner, ref in enumerate((fan, other)):
+        outs = pl.pallas_call(
+            functools.partial(finish_kernel, partner),
+            out_shape=(jax.ShapeDtypeStruct((NS, NC, NX, ROWS, 128), bf16), out, out, out),
+            in_specs=[VMEM] * 4 + [HBM] * len(outs),
+            out_specs=(HBM,) * 4,
+            input_output_aliases={4 + i: i for i in range(len(outs))},
+            scratch_shapes=[
+                pltpu.VMEM((3, NX * ROWS, 128), f32),
+                pltpu.SemaphoreType.DMA((NX,)),
+                pltpu.SemaphoreType.DMA((3,)),
+            ],
+            compiler_params=PARAMS,
+            cost_estimate=pl.CostEstimate(flops=1 << 18, bytes_accessed=3 << 19, transcendentals=0),
+            name="finish_partner" if partner else "finish_own",
+        )(ref, master, first, second, *outs)
+    weights, new_master, new_first, new_second = outs
     return (new_master.reshape(-1), new_first.reshape(-1), new_second.reshape(-1), weights.reshape(-1))
 
 

time: 104 us -> 102 us (0.981)
  other arithmetic: 1.37 us -> 0.08 us
    convert_element_type x1 -> x0, other arithmetic: 1.29 us -> none  [shards(): parts = (scaled(0).astype(f32) + got.astype(f32)).astype(bf16)]
  transfers between devices with their start and end apart: 2 -> 2, of which waited for: 1 -> 2; matrix products, arithmetic and copies ran while one was open for 0% -> 0% of each run, Pallas kernels for 2% -> 2%
where the time goes in v3:
time: 102 us; the launch traced here: 101 us
  blocking collectives  82.3 us (81%)
  starting transfers between devices  11.4 us (11%)
  Pallas kernels  5.67 us (6%)
    all_to_all x1, blocking collectives, shards(): parts = lax.all_to_all(parts, ('zl', 'zh'), 0, 0, tiled=True)  26.8 us
    all_to_all x1, blocking collectives, shards(): lax.all_to_all(weights, ('zl', 'y', 'zh'), 0, 0, tiled=True, axis_index_g...  18.9 us
    all_to_all x1, blocking collectives, shards(): parts = lax.all_to_all(parts, 'y', 0, 0, tiled=True)  14.6 us
    all_to_all x1, blocking collectives, shards(): parts = lax.all_to_all(parts, 'x', 0, 0, tiled=True)  12.4 us
    all_to_all x1, blocking collectives, shards(): fan = lax.all_to_all(fan, 'x', 0, 0, tiled=True)  9.48 us
    ppermute x1, starting transfers between devices, shards(): other = lax.ppermute(fan, 'c', swap)  8.81 us
    pallas_call x2, Pallas kernels, scaled(): pl.pallas_call(functools.partial(scale_kernel, core), out_shape=jax.Shape...  3.56 us
    ppermute x1, starting transfers between devices, shards(): got = lax.ppermute(scaled(1), 'c', swap)  2.58 us
  transfers between devices with their start and end apart: 2, of which 2 were waited for; matrix products, arithmetic and copies ran while one was open for 0% of the time, Pallas kernels for 2%

profile of v3, /device:TPU:193, one launch (start us, length us, event | category | flops | bytes accessed | tf_op | source)
XLA Modules:
  0.0 101.2 jit_solution(16876599149718034147)
XLA Ops:
  0.6 0.0 copy-start.3
  0.6 2.2 %scale_send.1 = bf16[4,8,2,32,128]{4,3,2,1,0:T(8,128)(2,1)} custom-call(s32[64]{0:T(128)} %ranks.3, f32[8,2,2,128,128]{4,3,2,1,0:T(8,128)} %bitcast.17), custom_call_target="tpu_custom_call" | custom-call | flops 262144 | bytes 1572864 | tf_op jit(solution)/shard_map/scale_send/pallas_call | solution.py:111
  2.8 2.6 %collective-permute-start = (bf16[4,8,2,32,128]{4,3,2,1,0:T(8,128)(2,1)}, bf16[4,8,2,32,128]{4,3,2,1,0:T(8,128)(2,1)S(1)}, u32[]{:S(2)}, u32[]{:S(2)}) collective-permute-start(bf16[4,8,2,32,128]{4,3,2,1,0:T(8,128)(2,1)} %scale_send.1), channel_id=1, source_target_pairs={{0,16},{16,0},{1,17},{17,1},{2,18},{18,2},{3,19},{19,3},{4,20},{20... | collective-permute-start | bytes 1572872 | tf_op jit(solution)/shard_map/ppermute | solution.py:138
  5.4 0.0 copy-done.3
  5.4 1.4 %scale_own.1.own = bf16[4,8,2,32,128]{4,3,2,1,0:T(8,128)(2,1)S(1)} custom-call(s32[64]{0:T(128)S(1)} %copy-done.3, f32[8,2,2,128,128]{4,3,2,1,0:T(8,128)} %bitcast.18), custom_call_target="tpu_custom_call" | custom-call | flops 262144 | bytes 1572864 | tf_op jit(solution)/shard_map/scale_own/pallas_call | solution.py:111
  6.8 0.0 copy-start
  6.8 0.0 copy-start.1
  6.8 0.0 copy-start.2
  6.9 0.3 collective-permute-done.got
  7.1 0.1 combine_kernel.1
  7.3 12.4 %all_to_all.25 = bf16[4,8,2,32,128]{4,3,2,1,0:T(8,128)(2,1)S(1)} all-to-all(bf16[4,8,2,32,128]{4,3,2,1,0:T(8,128)(2,1)S(1)} %combine_kernel.1), channel_id=1, replica_groups=mesh['x'=4,'zl'=8,'c'=2,'y'=8,'zh'=2] {'x'}, dimensions={0} | all-to-all | bytes 1048576 | tf_op jit(solution)/shard_map/all_to_all | solution.py:141
  19.7 0.1 reduce_sum.12
  19.8 14.6 %all_to_all.26.parts = bf16[8,2,32,128]{3,2,1,0:T(8,128)(2,1)S(1)} all-to-all(bf16[8,2,32,128]{3,2,1,0:T(8,128)(2,1)S(1)} %reduce_sum.12), channel_id=1, replica_groups=mesh['x'=4,'zl'=8,'c'=2,'y'=8,'zh'=2] {'y'}, dimensions={0} | all-to-all | bytes 262144 | tf_op jit(solution)/shard_map/all_to_all | solution.py:143
  34.5 26.8 %all_to_all.27.parts = bf16[16,32,128]{2,1,0:T(8,128)(2,1)S(1)} all-to-all(bf16[16,32,128]{2,1,0:T(8,128)(2,1)S(1)} %spread_kernel.1), channel_id=1, replica_groups=mesh['x'=4,'zl'=8,'c'=2,'y'=8,'zh'=2] {'zl','zh'}, dimensions={0} | all-to-all | bytes 262144 | tf_op jit(solution)/shard_map/all_to_all | solution.py:145
  61.3 0.0 copy-done
  61.3 0.0 copy-done.1
  61.3 0.0 copy-done.2
  61.3 0.1 update_kernel.1
  61.4 18.9 %all_to_all.28.weights = bf16[16,32,128]{2,1,0:T(8,128)(2,1)S(1)} all-to-all(bf16[16,32,128]{2,1,0:T(8,128)(2,1)S(1)} %get-tuple-element.14), channel_id=1, replica_groups={{0,225,2,227,4,229,6,231,8,233,10,235,12,237,14,239},{32,193,34,195,36,..., dimensions={0} | all-to-all | bytes 262144 | tf_op jit(solution)/shard_map/all_to_all | solution.py:154
  80.3 0.1 fan_kernel.1
  80.4 9.5 %all_to_all.29.refs_0_ = bf16[4,17,32,128]{3,2,1,0:T(8,128)(2,1)S(1)} all-to-all(bf16[4,17,32,128]{3,2,1,0:T(8,128)(2,1)S(1)} %fan_kernel.1), channel_id=1, replica_groups=mesh['x'=4,'zl'=8,'c'=2,'y'=8,'zh'=2] {'x'}, dimensions={0} | all-to-all | bytes 1114112 | tf_op jit(solution)/shard_map/all_to_all | solution.py:156
  89.9 8.8 %collective-permute-start.1 = (bf16[4,17,32,128]{3,2,1,0:T(8,128)(2,1)S(1)}, bf16[4,17,32,128]{3,2,1,0:T(8,128)(2,1)S(1)}, u32[]{:S(2)}, u32[]{:S(2)}) collective-permute-start(bf16[4,17,32,128]{3,2,1,0:T(8,128)(2,1)S(1)} %all_to_all.29.refs_0_), channel_id=1, source_target_pairs={{0,16},{16,0},{1,17},{17,1},{2,18},{18,2},{3,19},{19,3},{4,20},{20... | collective-permute-start | bytes 1671176 | tf_op jit(solution)/shard_map/ppermute | solution.py:157
  98.7 0.9 finish_own.1
  99.6 0.6 collective-permute-done.1.refs_0_
  100.3 0.9 finish_partner.1
  (1 shorter events, 0.0 us)
Async XLA Ops:
  0.6 4.8 %copy-start.3 = (s32[64]{0:T(128)S(1)}, s32[64]{0:T(128)}, u32[]{:S(2)}) copy-start(s32[64]{0:T(128)} %ranks.3) | copy-start | bytes 772
  2.8 4.3 %collective-permute-start = (bf16[4,8,2,32,128]{4,3,2,1,0:T(8,128)(2,1)}, bf16[4,8,2,32,128]{4,3,2,1,0:T(8,128)(2,1)S(1)}, u32[]{:S(2)}, u32[]{:S(2)}) collective-permute-start(bf16[4,8,2,32,128]{4,3,2,1,0:T(8,128)(2,1)} %scale_send.1), channel_id=1, source_target_pairs={{0,16},{16,0},{1,17},{17,1},{2,18},{18,2},{3,19},{19,3},{4,20},{20... | collective-permute-start | bytes 1572872 | tf_op jit(solution)/shard_map/ppermute | solution.py:138
  6.8 54.5 %copy-start = (f32[32768]{0:T(1024)S(1)}, f32[32768]{0:T(1024)}, u32[]{:S(2)}) copy-start(f32[32768]{0:T(1024)} %param.6) | copy-start | bytes 393220
  6.8 54.5 %copy-start.1 = (f32[32768]{0:T(1024)S(1)}, f32[32768]{0:T(1024)}, u32[]{:S(2)}) copy-start(f32[32768]{0:T(1024)} %param.7) | copy-start | bytes 393220
  6.8 54.5 %copy-start.2 = (f32[32768]{0:T(1024)S(1)}, f32[32768]{0:T(1024)}, u32[]{:S(2)}) copy-start(f32[32768]{0:T(1024)} %param.8) | copy-start | bytes 393220
  89.9 10.4 %collective-permute-start.1 = (bf16[4,17,32,128]{3,2,1,0:T(8,128)(2,1)S(1)}, bf16[4,17,32,128]{3,2,1,0:T(8,128)(2,1)S(1)}, u32[]{:S(2)}, u32[]{:S(2)}) collective-permute-start(bf16[4,17,32,128]{3,2,1,0:T(8,128)(2,1)S(1)} %all_to_all.29.refs_0_), channel_id=1, source_target_pairs={{0,16},{16,0},{1,17},{17,1},{2,18},{18,2},{3,19},{19,3},{4,20},{20... | collective-permute-start | bytes 1671176 | tf_op jit(solution)/shard_map/ppermute | solution.py:157

commit v4 on v3

--- a/solution.py
+++ b/solution.py
@@ -147,11 +147,12 @@
     weights, grad = local(
         update_kernel, (jax.ShapeDtypeStruct((NS, ROWS, 128), bf16), piece), parts, master, first, second
     )
-    mirrors = [
-        [(z % NZL) * NS + y * NZH + z // NZL for y in range(NY) for z in (low, NZ - 1 - low)]
+    pairs = [
+        [(z % NZL) * NS + y * NZH + z // NZL for y in range(NY) for z in (low, (low + far) % NZ)]
         for low in range(NZL)
+        for far in (NZL // 2 if low >= NZL // 2 else NZ - NZL // 2,)
     ]
-    weights = lax.all_to_all(weights, ("zl", "y", "zh"), 0, 0, tiled=True, axis_index_groups=mirrors)
+    weights = lax.all_to_all(weights, ("zl", "y", "zh"), 0, 0, tiled=True, axis_index_groups=pairs)
     fan = local(fan_kernel, jax.ShapeDtypeStruct((NX, NS + 1, ROWS, 128), bf16), weights, grad)
     fan = lax.all_to_all(fan, "x", 0, 0, tiled=True)
     other = lax.ppermute(fan, "c", swap)

time: 102 us -> 102 us (level)
  the two profiles are of different devices: /device:TPU:193 before, /device:TPU:1 now
where the time goes in v4:
time: 102 us
  blocking collectives  69.7 us (68%)
  starting transfers between devices  24.9 us (24%)
  Pallas kernels  5.67 us (6%)
    all_to_all x1, blocking collectives, shards(): parts = lax.all_to_all(parts, ('zl', 'zh'), 0, 0, tiled=True)  23.9 us
    ppermute x1, starting transfers between devices, shards(): got = lax.ppermute(scaled(1), 'c', swap)  16 us
    all_to_all x1, blocking collectives, shards(): lax.all_to_all(weights, ('zl', 'y', 'zh'), 0, 0, tiled=True, axis_index_g...  14.4 us
    all_to_all x1, blocking collectives, shards(): parts = lax.all_to_all(parts, 'x', 0, 0, tiled=True)  11.6 us
    all_to_all x1, blocking collectives, shards(): parts = lax.all_to_all(parts, 'y', 0, 0, tiled=True)  10.3 us
    all_to_all x1, blocking collectives, shards(): fan = lax.all_to_all(fan, 'x', 0, 0, tiled=True)  9.48 us
    ppermute x1, starting transfers between devices, shards(): other = lax.ppermute(fan, 'c', swap)  8.84 us
    pallas_call x2, Pallas kernels, scaled(): pl.pallas_call(functools.partial(scale_kernel, core), out_shape=jax.Shape...  3.56 us
  transfers between devices with their start and end apart: 2, of which 2 were waited for; matrix products, arithmetic and copies ran while one was open for 0% of the time, Pallas kernels for 2%

profile of v4, /device:TPU:1, one launch (start us, length us, event | category | flops | bytes accessed | tf_op | source)
XLA Modules:
  0.0 102.0 jit_solution(3561295600962524836)
XLA Ops:
  0.6 0.0 copy-start.3
  0.6 2.2 %scale_send.1 = bf16[4,8,2,32,128]{4,3,2,1,0:T(8,128)(2,1)} custom-call(s32[64]{0:T(128)} %ranks.3, f32[8,2,2,128,128]{4,3,2,1,0:T(8,128)} %bitcast.17), custom_call_target="tpu_custom_call" | custom-call | flops 262144 | bytes 1572864 | tf_op jit(solution)/shard_map/scale_send/pallas_call | solution.py:111
  2.8 16.0 %collective-permute-start = (bf16[4,8,2,32,128]{4,3,2,1,0:T(8,128)(2,1)}, bf16[4,8,2,32,128]{4,3,2,1,0:T(8,128)(2,1)S(1)}, u32[]{:S(2)}, u32[]{:S(2)}) collective-permute-start(bf16[4,8,2,32,128]{4,3,2,1,0:T(8,128)(2,1)} %scale_send.1), channel_id=1, source_target_pairs={{0,16},{16,0},{1,17},{17,1},{2,18},{18,2},{3,19},{19,3},{4,20},{20... | collective-permute-start | bytes 1572872 | tf_op jit(solution)/shard_map/ppermute | solution.py:138
  18.9 0.0 copy-done.3
  18.9 1.4 %scale_own.1.own = bf16[4,8,2,32,128]{4,3,2,1,0:T(8,128)(2,1)S(1)} custom-call(s32[64]{0:T(128)S(1)} %copy-done.3, f32[8,2,2,128,128]{4,3,2,1,0:T(8,128)} %bitcast.18), custom_call_target="tpu_custom_call" | custom-call | flops 262144 | bytes 1572864 | tf_op jit(solution)/shard_map/scale_own/pallas_call | solution.py:111
  20.3 0.0 copy-start
  20.3 0.0 copy-start.1
  20.3 0.0 copy-start.2
  20.3 0.3 collective-permute-done.got
  20.6 0.1 combine_kernel.1
  20.7 11.6 %all_to_all.25 = bf16[4,8,2,32,128]{4,3,2,1,0:T(8,128)(2,1)S(1)} all-to-all(bf16[4,8,2,32,128]{4,3,2,1,0:T(8,128)(2,1)S(1)} %combine_kernel.1), channel_id=1, replica_groups=mesh['x'=4,'zl'=8,'c'=2,'y'=8,'zh'=2] {'x'}, dimensions={0} | all-to-all | bytes 1048576 | tf_op jit(solution)/shard_map/all_to_all | solution.py:141
  32.3 0.1 reduce_sum.12
  32.4 10.3 %all_to_all.26.parts = bf16[8,2,32,128]{3,2,1,0:T(8,128)(2,1)S(1)} all-to-all(bf16[8,2,32,128]{3,2,1,0:T(8,128)(2,1)S(1)} %reduce_sum.12), channel_id=1, replica_groups=mesh['x'=4,'zl'=8,'c'=2,'y'=8,'zh'=2] {'y'}, dimensions={0} | all-to-all | bytes 262144 | tf_op jit(solution)/shard_map/all_to_all | solution.py:143
  42.8 23.9 %all_to_all.27.parts = bf16[16,32,128]{2,1,0:T(8,128)(2,1)S(1)} all-to-all(bf16[16,32,128]{2,1,0:T(8,128)(2,1)S(1)} %spread_kernel.1), channel_id=1, replica_groups=mesh['x'=4,'zl'=8,'c'=2,'y'=8,'zh'=2] {'zl','zh'}, dimensions={0} | all-to-all | bytes 262144 | tf_op jit(solution)/shard_map/all_to_all | solution.py:145
  66.7 0.0 copy-done
  66.7 0.0 copy-done.1
  66.7 0.0 copy-done.2
  66.7 0.1 update_kernel.1
  66.7 14.4 %all_to_all.28.weights = bf16[16,32,128]{2,1,0:T(8,128)(2,1)S(1)} all-to-all(bf16[16,32,128]{2,1,0:T(8,128)(2,1)S(1)} %get-tuple-element.14), channel_id=1, replica_groups={{0,129,2,131,4,133,6,135,8,137,10,139,12,141,14,143},{32,161,34,163,36,..., dimensions={0} | all-to-all | bytes 262144 | tf_op jit(solution)/shard_map/all_to_all | solution.py:155
  81.1 0.1 fan_kernel.1
  81.2 9.5 %all_to_all.29.refs_0_ = bf16[4,17,32,128]{3,2,1,0:T(8,128)(2,1)S(1)} all-to-all(bf16[4,17,32,128]{3,2,1,0:T(8,128)(2,1)S(1)} %fan_kernel.1), channel_id=1, replica_groups=mesh['x'=4,'zl'=8,'c'=2,'y'=8,'zh'=2] {'x'}, dimensions={0} | all-to-all | bytes 1114112 | tf_op jit(solution)/shard_map/all_to_all | solution.py:157
  90.7 8.8 %collective-permute-start.1 = (bf16[4,17,32,128]{3,2,1,0:T(8,128)(2,1)S(1)}, bf16[4,17,32,128]{3,2,1,0:T(8,128)(2,1)S(1)}, u32[]{:S(2)}, u32[]{:S(2)}) collective-permute-start(bf16[4,17,32,128]{3,2,1,0:T(8,128)(2,1)S(1)} %all_to_all.29.refs_0_), channel_id=1, source_target_pairs={{0,16},{16,0},{1,17},{17,1},{2,18},{18,2},{3,19},{19,3},{4,20},{20... | collective-permute-start | bytes 1671176 | tf_op jit(solution)/shard_map/ppermute | solution.py:158
  99.6 0.9 finish_own.1
  100.5 0.6 collective-permute-done.1.refs_0_
  101.1 0.9 finish_partner.1
  (1 shorter events, 0.0 us)
Async XLA Ops:
  0.6 18.2 %copy-start.3 = (s32[64]{0:T(128)S(1)}, s32[64]{0:T(128)}, u32[]{:S(2)}) copy-start(s32[64]{0:T(128)} %ranks.3) | copy-start | bytes 772
  2.8 17.8 %collective-permute-start = (bf16[4,8,2,32,128]{4,3,2,1,0:T(8,128)(2,1)}, bf16[4,8,2,32,128]{4,3,2,1,0:T(8,128)(2,1)S(1)}, u32[]{:S(2)}, u32[]{:S(2)}) collective-permute-start(bf16[4,8,2,32,128]{4,3,2,1,0:T(8,128)(2,1)} %scale_send.1), channel_id=1, source_target_pairs={{0,16},{16,0},{1,17},{17,1},{2,18},{18,2},{3,19},{19,3},{4,20},{20... | collective-permute-start | bytes 1572872 | tf_op jit(solution)/shard_map/ppermute | solution.py:138
  20.3 46.4 %copy-start = (f32[32768]{0:T(1024)S(1)}, f32[32768]{0:T(1024)}, u32[]{:S(2)}) copy-start(f32[32768]{0:T(1024)} %param.6) | copy-start | bytes 393220
  20.3 46.4 %copy-start.1 = (f32[32768]{0:T(1024)S(1)}, f32[32768]{0:T(1024)}, u32[]{:S(2)}) copy-start(f32[32768]{0:T(1024)} %param.7) | copy-start | bytes 393220
  20.3 46.4 %copy-start.2 = (f32[32768]{0:T(1024)S(1)}, f32[32768]{0:T(1024)}, u32[]{:S(2)}) copy-start(f32[32768]{0:T(1024)} %param.8) | copy-start | bytes 393220
  90.7 10.4 %collective-permute-start.1 = (bf16[4,17,32,128]{3,2,1,0:T(8,128)(2,1)S(1)}, bf16[4,17,32,128]{3,2,1,0:T(8,128)(2,1)S(1)}, u32[]{:S(2)}, u32[]{:S(2)}) collective-permute-start(bf16[4,17,32,128]{3,2,1,0:T(8,128)(2,1)S(1)} %all_to_all.29.refs_0_), channel_id=1, source_target_pairs={{0,16},{16,0},{1,17},{17,1},{2,18},{18,2},{3,19},{19,3},{4,20},{20... | collective-permute-start | bytes 1671176 | tf_op jit(solution)/shard_map/ppermute | solution.py:158

commit v5 on v3

--- a/solution.py
+++ b/solution.py
@@ -29,7 +29,7 @@
     return (new_master, new_first, new_second)
 
 
-def scale_kernel(core, ranks, grads, out, buf, rank, sem, rank_sem):
+def scale_kernel(core, ranks, grads, out, buf, rank, sem, rank_sem, *send):
     x, zl, c = lax.axis_index("x"), lax.axis_index("zl"), lax.axis_index("c")
     half = 1 - c if core else c
     copies = [pltpu.make_async_copy(grads.at[y, :, half], buf.at[y], sem.at[y]) for y in range(NY)]
@@ -40,11 +40,18 @@
     rank_copy.wait()
     outer = (x * NZL + zl) * NC + c
     weight = 1.0 + rank[outer].astype(f32) * (2.0 / 63.0)
+    stage = send[0] if core else out
+    sends = []
     for y in range(NY):
         copies[y].wait()
         for k in range(NX):
             for z in range(NZH):
-                out[k, y, z] = (buf[y, z, pl.ds(k * ROWS, ROWS)] * weight).astype(bf16)
+                stage[k, y, z] = (buf[y, z, pl.ds(k * ROWS, ROWS)] * weight).astype(bf16)
+        if core:
+            sends.append(pltpu.make_async_copy(stage.at[:, y], out.at[:, y], send[1].at[y]))
+            sends[-1].start()
+    for copy in sends:
+        copy.wait()
 
 
 def combine_kernel(own, got, out):
@@ -54,8 +61,8 @@
 
 def spread_kernel(parts, out):
     total = parts[0].astype(f32)
-    for y in range(1, NY):
-        total += parts[y].astype(f32)
+    for xy in range(1, NX * NY):
+        total += parts[xy].astype(f32)
     total = total.astype(bf16)
     for z in range(NZL):
         for zh in range(NZH):
@@ -107,18 +114,21 @@
     master, first, second = (a.reshape(shard) for a in (master, first_moment, second_moment))
     grads = grads.reshape((NY, NZH, NC, NX * ROWS, 128))
 
+    half = (NX, NY, NZH, ROWS, 128)
+
     def scaled(core):
         return pl.pallas_call(
             functools.partial(scale_kernel, core),
-            out_shape=jax.ShapeDtypeStruct((NX, NY, NZH, ROWS, 128), bf16),
+            out_shape=jax.ShapeDtypeStruct(half, bf16),
             in_specs=[HBM, HBM],
-            out_specs=VMEM,
+            out_specs=HBM if core else VMEM,
             scratch_shapes=[
                 pltpu.VMEM((NY, NZH, NX * ROWS, 128), f32),
                 pltpu.SMEM((64,), jnp.int32),
                 pltpu.SemaphoreType.DMA((NY,)),
                 pltpu.SemaphoreType.DMA,
-            ],
+            ]
+            + [pltpu.VMEM(half, bf16), pltpu.SemaphoreType.DMA((NY,))] * core,
             compiler_params=pltpu.CompilerParams(vmem_limit_bytes=(60 if core else 52) << 20),
             cost_estimate=pl.CostEstimate(flops=1 << 18, bytes_accessed=3 << 19, transcendentals=0),
             name="scale_send" if core else "scale_own",
@@ -136,11 +146,9 @@
 
     swap = [(0, 1), (1, 0)]
     got = lax.ppermute(scaled(1), "c", swap)
-    half = jax.ShapeDtypeStruct((NX, NY, NZH, ROWS, 128), bf16)
-    parts = local(combine_kernel, half, scaled(0), got)
-    parts = lax.all_to_all(parts, "x", 0, 0, tiled=True)
-    parts = jnp.sum(parts.astype(f32), axis=0).astype(bf16)
-    parts = lax.all_to_all(parts, "y", 0, 0, tiled=True)
+    parts = local(combine_kernel, jax.ShapeDtypeStruct(half, bf16), scaled(0), got)
+    parts = parts.reshape((NX * NY, NZH, ROWS, 128))
+    parts = lax.all_to_all(parts, ("x", "y"), 0, 0, tiled=True)
     parts = local(spread_kernel, jax.ShapeDtypeStruct((NZ, ROWS, 128), bf16), parts)
     parts = lax.all_to_all(parts, ("zl", "zh"), 0, 0, tiled=True)
     piece = jax.ShapeDtypeStruct((ROWS, 128), bf16)

time: 102 us -> 102 us (level)
  blocking collectives: 82.3 us -> 83.7 us
    all_to_all x1, blocking collectives: 18.9 us -> 23.3 us  [shards(): lax.all_to_all(weights, ('zl', 'y', 'zh'), 0, 0, tiled=True, axis_index_g...]
    all_to_all x2 -> x1, blocking collectives: 27.1 us -> 23.7 us  [shards(): parts = lax.all_to_all(parts, ('x', 'y'), 0, 0, tiled=True)]
where the time goes in v5:
time: 102 us
  blocking collectives  83.7 us (82%)
  starting transfers between devices  10.9 us (11%)
  Pallas kernels  5.62 us (6%)
    all_to_all x1, blocking collectives, shards(): parts = lax.all_to_all(parts, ('zl', 'zh'), 0, 0, tiled=True)  26.8 us
    all_to_all x1, blocking collectives, shards(): parts = lax.all_to_all(parts, ('x', 'y'), 0, 0, tiled=True)  23.7 us
    all_to_all x1, blocking collectives, shards(): lax.all_to_all(weights, ('zl', 'y', 'zh'), 0, 0, tiled=True, axis_index_g...  23.3 us
    all_to_all x1, blocking collectives, shards(): fan = lax.all_to_all(fan, 'x', 0, 0, tiled=True)  9.9 us
    ppermute x1, starting transfers between devices, shards(): other = lax.ppermute(fan, 'c', swap)  8.31 us
    pallas_call x2, Pallas kernels, scaled(): pl.pallas_call(functools.partial(scale_kernel, core), out_shape=jax.Shape...  3.47 us
    ppermute x1, starting transfers between devices, shards(): got = lax.ppermute(scaled(1), 'c', swap)  2.58 us
  transfers between devices with their start and end apart: 2, of which 2 were waited for; matrix products, arithmetic and copies ran while one was open for 0% of the time, Pallas kernels for 2%

profile of v5, /device:TPU:193, one launch (start us, length us, event | category | flops | bytes accessed | tf_op | source)
XLA Modules:
  0.0 101.9 jit_solution(9140613725818003948)
XLA Ops:
  0.6 0.0 copy-start.3
  0.6 2.1 %scale_send.1 = bf16[4,8,2,32,128]{4,3,2,1,0:T(8,128)(2,1)} custom-call(s32[64]{0:T(128)} %ranks.3, f32[8,2,2,128,128]{4,3,2,1,0:T(8,128)} %bitcast.19), custom_call_target="tpu_custom_call" | custom-call | flops 262144 | bytes 1572864 | tf_op jit(solution)/shard_map/scale_send/pallas_call | solution.py:120
  2.7 2.6 %collective-permute-start = (bf16[4,8,2,32,128]{4,3,2,1,0:T(8,128)(2,1)}, bf16[4,8,2,32,128]{4,3,2,1,0:T(8,128)(2,1)S(1)}, u32[]{:S(2)}, u32[]{:S(2)}) collective-permute-start(bf16[4,8,2,32,128]{4,3,2,1,0:T(8,128)(2,1)} %scale_send.1), channel_id=1, source_target_pairs={{0,16},{16,0},{1,17},{17,1},{2,18},{18,2},{3,19},{19,3},{4,20},{20... | collective-permute-start | bytes 1572872 | tf_op jit(solution)/shard_map/ppermute | solution.py:148
  5.3 0.0 copy-done.3
  5.3 1.4 %scale_own.1.own = bf16[4,8,2,32,128]{4,3,2,1,0:T(8,128)(2,1)S(1)} custom-call(s32[64]{0:T(128)S(1)} %copy-done.3, f32[8,2,2,128,128]{4,3,2,1,0:T(8,128)} %bitcast.20), custom_call_target="tpu_custom_call" | custom-call | flops 262144 | bytes 1572864 | tf_op jit(solution)/shard_map/scale_own/pallas_call | solution.py:120
  6.7 0.0 copy-start
  6.7 0.0 copy-start.1
  6.7 0.0 copy-start.2
  6.8 0.3 collective-permute-done.got
  7.0 0.1 combine_kernel.1
  7.2 23.7 %all_to_all.20.parts = bf16[32,2,32,128]{3,2,1,0:T(8,128)(2,1)S(1)} all-to-all(bf16[32,2,32,128]{3,2,1,0:T(8,128)(2,1)S(1)} %bitcast.9), channel_id=1, replica_groups=mesh['x'=4,'zl'=8,'c'=2,'y'=8,'zh'=2] {'x','y'}, dimensions={0} | all-to-all | bytes 1048576 | tf_op jit(solution)/shard_map/all_to_all | solution.py:151
  30.8 0.1 spread_kernel.1
  30.9 26.8 %all_to_all.21.parts = bf16[16,32,128]{2,1,0:T(8,128)(2,1)S(1)} all-to-all(bf16[16,32,128]{2,1,0:T(8,128)(2,1)S(1)} %spread_kernel.1), channel_id=1, replica_groups=mesh['x'=4,'zl'=8,'c'=2,'y'=8,'zh'=2] {'zl','zh'}, dimensions={0} | all-to-all | bytes 262144 | tf_op jit(solution)/shard_map/all_to_all | solution.py:153
  57.8 0.0 copy-done
  57.8 0.0 copy-done.1
  57.8 0.0 copy-done.2
  57.8 0.1 update_kernel.1
  57.8 23.3 %all_to_all.22.weights = bf16[16,32,128]{2,1,0:T(8,128)(2,1)S(1)} all-to-all(bf16[16,32,128]{2,1,0:T(8,128)(2,1)S(1)} %get-tuple-element.14), channel_id=1, replica_groups={{0,225,2,227,4,229,6,231,8,233,10,235,12,237,14,239},{32,193,34,195,36,..., dimensions={0} | all-to-all | bytes 262144 | tf_op jit(solution)/shard_map/all_to_all | solution.py:162
  81.2 0.1 fan_kernel.1
  81.2 9.9 %all_to_all.23.refs_0_ = bf16[4,17,32,128]{3,2,1,0:T(8,128)(2,1)S(1)} all-to-all(bf16[4,17,32,128]{3,2,1,0:T(8,128)(2,1)S(1)} %fan_kernel.1), channel_id=1, replica_groups=mesh['x'=4,'zl'=8,'c'=2,'y'=8,'zh'=2] {'x'}, dimensions={0} | all-to-all | bytes 1114112 | tf_op jit(solution)/shard_map/all_to_all | solution.py:164
  91.1 8.3 %collective-permute-start.1 = (bf16[4,17,32,128]{3,2,1,0:T(8,128)(2,1)S(1)}, bf16[4,17,32,128]{3,2,1,0:T(8,128)(2,1)S(1)}, u32[]{:S(2)}, u32[]{:S(2)}) collective-permute-start(bf16[4,17,32,128]{3,2,1,0:T(8,128)(2,1)S(1)} %all_to_all.23.refs_0_), channel_id=1, source_target_pairs={{0,16},{16,0},{1,17},{17,1},{2,18},{18,2},{3,19},{19,3},{4,20},{20... | collective-permute-start | bytes 1671176 | tf_op jit(solution)/shard_map/ppermute | solution.py:165
  99.4 0.9 finish_own.1
  100.4 0.6 collective-permute-done.1.refs_0_
  101.0 0.9 finish_partner.1
Async XLA Ops:
  0.6 4.7 %copy-start.3 = (s32[64]{0:T(128)S(1)}, s32[64]{0:T(128)}, u32[]{:S(2)}) copy-start(s32[64]{0:T(128)} %ranks.3) | copy-start | bytes 772
  2.7 4.3 %collective-permute-start = (bf16[4,8,2,32,128]{4,3,2,1,0:T(8,128)(2,1)}, bf16[4,8,2,32,128]{4,3,2,1,0:T(8,128)(2,1)S(1)}, u32[]{:S(2)}, u32[]{:S(2)}) collective-permute-start(bf16[4,8,2,32,128]{4,3,2,1,0:T(8,128)(2,1)} %scale_send.1), channel_id=1, source_target_pairs={{0,16},{16,0},{1,17},{17,1},{2,18},{18,2},{3,19},{19,3},{4,20},{20... | collective-permute-start | bytes 1572872 | tf_op jit(solution)/shard_map/ppermute | solution.py:148
  6.7 51.0 %copy-start = (f32[32768]{0:T(1024)S(1)}, f32[32768]{0:T(1024)}, u32[]{:S(2)}) copy-start(f32[32768]{0:T(1024)} %param.6) | copy-start | bytes 393220
  6.7 51.0 %copy-start.1 = (f32[32768]{0:T(1024)S(1)}, f32[32768]{0:T(1024)}, u32[]{:S(2)}) copy-start(f32[32768]{0:T(1024)} %param.7) | copy-start | bytes 393220
  6.7 51.0 %copy-start.2 = (f32[32768]{0:T(1024)S(1)}, f32[32768]{0:T(1024)}, u32[]{:S(2)}) copy-start(f32[32768]{0:T(1024)} %param.8) | copy-start | bytes 393220
  91.1 9.9 %collective-permute-start.1 = (bf16[4,17,32,128]{3,2,1,0:T(8,128)(2,1)S(1)}, bf16[4,17,32,128]{3,2,1,0:T(8,128)(2,1)S(1)}, u32[]{:S(2)}, u32[]{:S(2)}) collective-permute-start(bf16[4,17,32,128]{3,2,1,0:T(8,128)(2,1)S(1)} %all_to_all.23.refs_0_), channel_id=1, source_target_pairs={{0,16},{16,0},{1,17},{17,1},{2,18},{18,2},{3,19},{19,3},{4,20},{20... | collective-permute-start | bytes 1671176 | tf_op jit(solution)/shard_map/ppermute | solution.py:165

commit v6 on v5

--- a/solution.py
+++ b/solution.py
@@ -61,8 +61,8 @@
 
 def spread_kernel(parts, out):
     total = parts[0].astype(f32)
-    for xy in range(1, NX * NY):
-        total += parts[xy].astype(f32)
+    for y in range(1, NY):
+        total += parts[y].astype(f32)
     total = total.astype(bf16)
     for z in range(NZL):
         for zh in range(NZH):
@@ -147,8 +147,9 @@
     swap = [(0, 1), (1, 0)]
     got = lax.ppermute(scaled(1), "c", swap)
     parts = local(combine_kernel, jax.ShapeDtypeStruct(half, bf16), scaled(0), got)
-    parts = parts.reshape((NX * NY, NZH, ROWS, 128))
-    parts = lax.all_to_all(parts, ("x", "y"), 0, 0, tiled=True)
+    parts = lax.all_to_all(parts, "x", 0, 0, tiled=True)
+    parts = jnp.sum(parts.astype(f32), axis=0).astype(bf16)
+    parts = lax.all_to_all(parts, "y", 0, 0, tiled=True)
     parts = local(spread_kernel, jax.ShapeDtypeStruct((NZ, ROWS, 128), bf16), parts)
     parts = lax.all_to_all(parts, ("zl", "zh"), 0, 0, tiled=True)
     piece = jax.ShapeDtypeStruct((ROWS, 128), bf16)

time: 102 us -> 101 us (level)
  blocking collectives: 83.7 us -> 82.3 us
    all_to_all x1, blocking collectives: 23.3 us -> 18.9 us  [shards(): lax.all_to_all(weights, ('zl', 'y', 'zh'), 0, 0, tiled=True, axis_index_g...]
    all_to_all x1 -> x2, blocking collectives: 23.7 us -> 27.1 us  [the longest x1 14.6 us: shards(): parts = lax.all_to_all(parts, 'y', 0, 0, tiled=True)]
where the time goes in v6:
time: 101 us
  blocking collectives  82.3 us (81%)
  starting transfers between devices  11.4 us (11%)
  Pallas kernels  5.58 us (6%)
    all_to_all x1, blocking collectives, shards(): parts = lax.all_to_all(parts, ('zl', 'zh'), 0, 0, tiled=True)  26.8 us
    all_to_all x1, blocking collectives, shards(): lax.all_to_all(weights, ('zl', 'y', 'zh'), 0, 0, tiled=True, axis_index_g...  18.9 us
    all_to_all x1, blocking collectives, shards(): parts = lax.all_to_all(parts, 'y', 0, 0, tiled=True)  14.6 us
    all_to_all x1, blocking collectives, shards(): parts = lax.all_to_all(parts, 'x', 0, 0, tiled=True)  12.4 us
    all_to_all x1, blocking collectives, shards(): fan = lax.all_to_all(fan, 'x', 0, 0, tiled=True)  9.48 us
    ppermute x1, starting transfers between devices, shards(): other = lax.ppermute(fan, 'c', swap)  8.81 us
    pallas_call x2, Pallas kernels, scaled(): pl.pallas_call(functools.partial(scale_kernel, core), out_shape=jax.Shape...  3.47 us
    ppermute x1, starting transfers between devices, shards(): got = lax.ppermute(scaled(1), 'c', swap)  2.58 us
  transfers between devices with their start and end apart: 2, of which 2 were waited for; matrix products, arithmetic and copies ran while one was open for 0% of the time, Pallas kernels for 2%

profile of v6, /device:TPU:193, one launch (start us, length us, event | category | flops | bytes accessed | tf_op | source)
XLA Modules:
  0.0 101.1 jit_solution(13353263662798702498)
XLA Ops:
  0.6 0.0 copy-start.3
  0.6 2.1 %scale_send.1 = bf16[4,8,2,32,128]{4,3,2,1,0:T(8,128)(2,1)} custom-call(s32[64]{0:T(128)} %ranks.3, f32[8,2,2,128,128]{4,3,2,1,0:T(8,128)} %bitcast.17), custom_call_target="tpu_custom_call" | custom-call | flops 262144 | bytes 1572864 | tf_op jit(solution)/shard_map/scale_send/pallas_call | solution.py:120
  2.7 2.6 %collective-permute-start = (bf16[4,8,2,32,128]{4,3,2,1,0:T(8,128)(2,1)}, bf16[4,8,2,32,128]{4,3,2,1,0:T(8,128)(2,1)S(1)}, u32[]{:S(2)}, u32[]{:S(2)}) collective-permute-start(bf16[4,8,2,32,128]{4,3,2,1,0:T(8,128)(2,1)} %scale_send.1), channel_id=1, source_target_pairs={{0,16},{16,0},{1,17},{17,1},{2,18},{18,2},{3,19},{19,3},{4,20},{20... | collective-permute-start | bytes 1572872 | tf_op jit(solution)/shard_map/ppermute | solution.py:148
  5.3 0.0 copy-done.3
  5.3 1.4 %scale_own.1.own = bf16[4,8,2,32,128]{4,3,2,1,0:T(8,128)(2,1)S(1)} custom-call(s32[64]{0:T(128)S(1)} %copy-done.3, f32[8,2,2,128,128]{4,3,2,1,0:T(8,128)} %bitcast.18), custom_call_target="tpu_custom_call" | custom-call | flops 262144 | bytes 1572864 | tf_op jit(solution)/shard_map/scale_own/pallas_call | solution.py:120
  6.7 0.0 copy-start
  6.7 0.0 copy-start.1
  6.7 0.0 copy-start.2
  6.8 0.3 collective-permute-done.got
  7.0 0.1 combine_kernel.1
  7.2 12.4 %all_to_all.25 = bf16[4,8,2,32,128]{4,3,2,1,0:T(8,128)(2,1)S(1)} all-to-all(bf16[4,8,2,32,128]{4,3,2,1,0:T(8,128)(2,1)S(1)} %combine_kernel.1), channel_id=1, replica_groups=mesh['x'=4,'zl'=8,'c'=2,'y'=8,'zh'=2] {'x'}, dimensions={0} | all-to-all | bytes 1048576 | tf_op jit(solution)/shard_map/all_to_all | solution.py:150
  19.6 0.1 reduce_sum.12
  19.7 14.6 %all_to_all.26.parts = bf16[8,2,32,128]{3,2,1,0:T(8,128)(2,1)S(1)} all-to-all(bf16[8,2,32,128]{3,2,1,0:T(8,128)(2,1)S(1)} %reduce_sum.12), channel_id=1, replica_groups=mesh['x'=4,'zl'=8,'c'=2,'y'=8,'zh'=2] {'y'}, dimensions={0} | all-to-all | bytes 262144 | tf_op jit(solution)/shard_map/all_to_all | solution.py:152
  34.4 26.8 %all_to_all.27.parts = bf16[16,32,128]{2,1,0:T(8,128)(2,1)S(1)} all-to-all(bf16[16,32,128]{2,1,0:T(8,128)(2,1)S(1)} %spread_kernel.1), channel_id=1, replica_groups=mesh['x'=4,'zl'=8,'c'=2,'y'=8,'zh'=2] {'zl','zh'}, dimensions={0} | all-to-all | bytes 262144 | tf_op jit(solution)/shard_map/all_to_all | solution.py:154
  61.2 0.0 copy-done
  61.2 0.0 copy-done.1
  61.2 0.0 copy-done.2
  61.2 0.1 update_kernel.1
  61.3 18.9 %all_to_all.28.weights = bf16[16,32,128]{2,1,0:T(8,128)(2,1)S(1)} all-to-all(bf16[16,32,128]{2,1,0:T(8,128)(2,1)S(1)} %get-tuple-element.14), channel_id=1, replica_groups={{0,225,2,227,4,229,6,231,8,233,10,235,12,237,14,239},{32,193,34,195,36,..., dimensions={0} | all-to-all | bytes 262144 | tf_op jit(solution)/shard_map/all_to_all | solution.py:163
  80.2 0.1 fan_kernel.1
  80.3 9.5 %all_to_all.29.refs_0_ = bf16[4,17,32,128]{3,2,1,0:T(8,128)(2,1)S(1)} all-to-all(bf16[4,17,32,128]{3,2,1,0:T(8,128)(2,1)S(1)} %fan_kernel.1), channel_id=1, replica_groups=mesh['x'=4,'zl'=8,'c'=2,'y'=8,'zh'=2] {'x'}, dimensions={0} | all-to-all | bytes 1114112 | tf_op jit(solution)/shard_map/all_to_all | solution.py:165
  89.8 8.8 %collective-permute-start.1 = (bf16[4,17,32,128]{3,2,1,0:T(8,128)(2,1)S(1)}, bf16[4,17,32,128]{3,2,1,0:T(8,128)(2,1)S(1)}, u32[]{:S(2)}, u32[]{:S(2)}) collective-permute-start(bf16[4,17,32,128]{3,2,1,0:T(8,128)(2,1)S(1)} %all_to_all.29.refs_0_), channel_id=1, source_target_pairs={{0,16},{16,0},{1,17},{17,1},{2,18},{18,2},{3,19},{19,3},{4,20},{20... | collective-permute-start | bytes 1671176 | tf_op jit(solution)/shard_map/ppermute | solution.py:166
  98.6 0.9 finish_own.1
  99.5 0.6 collective-permute-done.1.refs_0_
  100.2 0.9 finish_partner.1
  (1 shorter events, 0.0 us)
Async XLA Ops:
  0.6 4.7 %copy-start.3 = (s32[64]{0:T(128)S(1)}, s32[64]{0:T(128)}, u32[]{:S(2)}) copy-start(s32[64]{0:T(128)} %ranks.3) | copy-start | bytes 772
  2.7 4.3 %collective-permute-start = (bf16[4,8,2,32,128]{4,3,2,1,0:T(8,128)(2,1)}, bf16[4,8,2,32,128]{4,3,2,1,0:T(8,128)(2,1)S(1)}, u32[]{:S(2)}, u32[]{:S(2)}) collective-permute-start(bf16[4,8,2,32,128]{4,3,2,1,0:T(8,128)(2,1)} %scale_send.1), channel_id=1, source_target_pairs={{0,16},{16,0},{1,17},{17,1},{2,18},{18,2},{3,19},{19,3},{4,20},{20... | collective-permute-start | bytes 1572872 | tf_op jit(solution)/shard_map/ppermute | solution.py:148
  6.7 54.5 %copy-start = (f32[32768]{0:T(1024)S(1)}, f32[32768]{0:T(1024)}, u32[]{:S(2)}) copy-start(f32[32768]{0:T(1024)} %param.6) | copy-start | bytes 393220
  6.7 54.5 %copy-start.1 = (f32[32768]{0:T(1024)S(1)}, f32[32768]{0:T(1024)}, u32[]{:S(2)}) copy-start(f32[32768]{0:T(1024)} %param.7) | copy-start | bytes 393220
  6.7 54.5 %copy-start.2 = (f32[32768]{0:T(1024)S(1)}, f32[32768]{0:T(1024)}, u32[]{:S(2)}) copy-start(f32[32768]{0:T(1024)} %param.8) | copy-start | bytes 393220
  89.8 10.4 %collective-permute-start.1 = (bf16[4,17,32,128]{3,2,1,0:T(8,128)(2,1)S(1)}, bf16[4,17,32,128]{3,2,1,0:T(8,128)(2,1)S(1)}, u32[]{:S(2)}, u32[]{:S(2)}) collective-permute-start(bf16[4,17,32,128]{3,2,1,0:T(8,128)(2,1)S(1)} %all_to_all.29.refs_0_), channel_id=1, source_target_pairs={{0,16},{16,0},{1,17},{17,1},{2,18},{18,2},{3,19},{19,3},{4,20},{20... | collective-permute-start | bytes 1671176 | tf_op jit(solution)/shard_map/ppermute | solution.py:166

commit v7 on v3

--- a/solution.py
+++ b/solution.py
@@ -57,9 +57,8 @@
     for y in range(1, NY):
         total += parts[y].astype(f32)
     total = total.astype(bf16)
-    for z in range(NZL):
-        for zh in range(NZH):
-            out[z * NZH + zh] = total[zh]
+    for z in range(NZ):
+        out[z] = total[z // NZL]
 
 
 def update_kernel(parts, master, first, second, weights, grad):
@@ -142,7 +141,8 @@
     parts = jnp.sum(parts.astype(f32), axis=0).astype(bf16)
     parts = lax.all_to_all(parts, "y", 0, 0, tiled=True)
     parts = local(spread_kernel, jax.ShapeDtypeStruct((NZ, ROWS, 128), bf16), parts)
-    parts = lax.all_to_all(parts, ("zl", "zh"), 0, 0, tiled=True)
+    ring = [[(z % NZL) * NZH + z // NZL for z in range(NZ)]]
+    parts = lax.all_to_all(parts, ("zl", "zh"), 0, 0, tiled=True, axis_index_groups=ring)
     piece = jax.ShapeDtypeStruct((ROWS, 128), bf16)
     weights, grad = local(
         update_kernel, (jax.ShapeDtypeStruct((NS, ROWS, 128), bf16), piece), parts, master, first, second

time: 102 us -> 101 us (level)
  no operation moved by 1% of the time
where the time goes in v7:
time: 101 us
  blocking collectives  81.9 us (81%)
  starting transfers between devices  11.5 us (11%)
  Pallas kernels  5.67 us (6%)
    all_to_all x1, blocking collectives, shards(): lax.all_to_all(parts, ('zl', 'zh'), 0, 0, tiled=True, axis_index_groups=r...  26.5 us
    all_to_all x1, blocking collectives, shards(): lax.all_to_all(weights, ('zl', 'y', 'zh'), 0, 0, tiled=True, axis_index_g...  18.8 us
    all_to_all x1, blocking collectives, shards(): parts = lax.all_to_all(parts, 'y', 0, 0, tiled=True)  14.6 us
    all_to_all x1, blocking collectives, shards(): parts = lax.all_to_all(parts, 'x', 0, 0, tiled=True)  12.4 us
    all_to_all x1, blocking collectives, shards(): fan = lax.all_to_all(fan, 'x', 0, 0, tiled=True)  9.48 us
    ppermute x1, starting transfers between devices, shards(): other = lax.ppermute(fan, 'c', swap)  8.95 us
    pallas_call x2, Pallas kernels, scaled(): pl.pallas_call(functools.partial(scale_kernel, core), out_shape=jax.Shape...  3.56 us
    ppermute x1, starting transfers between devices, shards(): got = lax.ppermute(scaled(1), 'c', swap)  2.58 us
  transfers between devices with their start and end apart: 2, of which 2 were waited for; matrix products, arithmetic and copies ran while one was open for 0% of the time, Pallas kernels for 2%

profile of v7, /device:TPU:193, one launch (start us, length us, event | category | flops | bytes accessed | tf_op | source)
XLA Modules:
  0.0 100.8 jit_solution(14571253527394918517)
XLA Ops:
  0.6 0.0 copy-start.3
  0.6 2.2 %scale_send.1 = bf16[4,8,2,32,128]{4,3,2,1,0:T(8,128)(2,1)} custom-call(s32[64]{0:T(128)} %ranks.3, f32[8,2,2,128,128]{4,3,2,1,0:T(8,128)} %bitcast.17), custom_call_target="tpu_custom_call" | custom-call | flops 262144 | bytes 1572864 | tf_op jit(solution)/shard_map/scale_send/pallas_call | solution.py:110
  2.8 2.6 %collective-permute-start = (bf16[4,8,2,32,128]{4,3,2,1,0:T(8,128)(2,1)}, bf16[4,8,2,32,128]{4,3,2,1,0:T(8,128)(2,1)S(1)}, u32[]{:S(2)}, u32[]{:S(2)}) collective-permute-start(bf16[4,8,2,32,128]{4,3,2,1,0:T(8,128)(2,1)} %scale_send.1), channel_id=1, source_target_pairs={{0,16},{16,0},{1,17},{17,1},{2,18},{18,2},{3,19},{19,3},{4,20},{20... | collective-permute-start | bytes 1572872 | tf_op jit(solution)/shard_map/ppermute | solution.py:137
  5.4 0.0 copy-done.3
  5.4 1.4 %scale_own.1.own = bf16[4,8,2,32,128]{4,3,2,1,0:T(8,128)(2,1)S(1)} custom-call(s32[64]{0:T(128)S(1)} %copy-done.3, f32[8,2,2,128,128]{4,3,2,1,0:T(8,128)} %bitcast.18), custom_call_target="tpu_custom_call" | custom-call | flops 262144 | bytes 1572864 | tf_op jit(solution)/shard_map/scale_own/pallas_call | solution.py:110
  6.8 0.0 copy-start
  6.8 0.0 copy-start.1
  6.8 0.0 copy-start.2
  6.9 0.3 collective-permute-done.got
  7.1 0.1 combine_kernel.1
  7.3 12.4 %all_to_all.25 = bf16[4,8,2,32,128]{4,3,2,1,0:T(8,128)(2,1)S(1)} all-to-all(bf16[4,8,2,32,128]{4,3,2,1,0:T(8,128)(2,1)S(1)} %combine_kernel.1), channel_id=1, replica_groups=mesh['x'=4,'zl'=8,'c'=2,'y'=8,'zh'=2] {'x'}, dimensions={0} | all-to-all | bytes 1048576 | tf_op jit(solution)/shard_map/all_to_all | solution.py:140
  19.7 0.1 reduce_sum.12
  19.8 14.6 %all_to_all.26.parts = bf16[8,2,32,128]{3,2,1,0:T(8,128)(2,1)S(1)} all-to-all(bf16[8,2,32,128]{3,2,1,0:T(8,128)(2,1)S(1)} %reduce_sum.12), channel_id=1, replica_groups=mesh['x'=4,'zl'=8,'c'=2,'y'=8,'zh'=2] {'y'}, dimensions={0} | all-to-all | bytes 262144 | tf_op jit(solution)/shard_map/all_to_all | solution.py:142
  34.5 26.5 %all_to_all.27.parts = bf16[16,32,128]{2,1,0:T(8,128)(2,1)S(1)} all-to-all(bf16[16,32,128]{2,1,0:T(8,128)(2,1)S(1)} %spread_kernel.1), channel_id=1, replica_groups={{0,32,64,96,128,160,192,224,1,33,65,97,129,161,193,225},{2,34,66,98,130..., dimensions={0} | all-to-all | bytes 262144 | tf_op jit(solution)/shard_map/all_to_all | solution.py:145
  61.0 0.0 copy-done
  61.0 0.0 copy-done.1
  61.0 0.0 copy-done.2
  61.0 0.1 update_kernel.1
  61.1 18.8 %all_to_all.28.weights = bf16[16,32,128]{2,1,0:T(8,128)(2,1)S(1)} all-to-all(bf16[16,32,128]{2,1,0:T(8,128)(2,1)S(1)} %get-tuple-element.14), channel_id=1, replica_groups={{0,225,2,227,4,229,6,231,8,233,10,235,12,237,14,239},{32,193,34,195,36,..., dimensions={0} | all-to-all | bytes 262144 | tf_op jit(solution)/shard_map/all_to_all | solution.py:154
  79.8 0.1 fan_kernel.1
  79.9 9.5 %all_to_all.29.refs_0_ = bf16[4,17,32,128]{3,2,1,0:T(8,128)(2,1)S(1)} all-to-all(bf16[4,17,32,128]{3,2,1,0:T(8,128)(2,1)S(1)} %fan_kernel.1), channel_id=1, replica_groups=mesh['x'=4,'zl'=8,'c'=2,'y'=8,'zh'=2] {'x'}, dimensions={0} | all-to-all | bytes 1114112 | tf_op jit(solution)/shard_map/all_to_all | solution.py:156
  89.4 8.9 %collective-permute-start.1 = (bf16[4,17,32,128]{3,2,1,0:T(8,128)(2,1)S(1)}, bf16[4,17,32,128]{3,2,1,0:T(8,128)(2,1)S(1)}, u32[]{:S(2)}, u32[]{:S(2)}) collective-permute-start(bf16[4,17,32,128]{3,2,1,0:T(8,128)(2,1)S(1)} %all_to_all.29.refs_0_), channel_id=1, source_target_pairs={{0,16},{16,0},{1,17},{17,1},{2,18},{18,2},{3,19},{19,3},{4,20},{20... | collective-permute-start | bytes 1671176 | tf_op jit(solution)/shard_map/ppermute | solution.py:157
  98.3 0.9 finish_own.1
  99.3 0.6 collective-permute-done.1.refs_0_
  99.9 0.9 finish_partner.1
  (1 shorter events, 0.0 us)
Async XLA Ops:
  0.6 4.8 %copy-start.3 = (s32[64]{0:T(128)S(1)}, s32[64]{0:T(128)}, u32[]{:S(2)}) copy-start(s32[64]{0:T(128)} %ranks.3) | copy-start | bytes 772
  2.8 4.3 %collective-permute-start = (bf16[4,8,2,32,128]{4,3,2,1,0:T(8,128)(2,1)}, bf16[4,8,2,32,128]{4,3,2,1,0:T(8,128)(2,1)S(1)}, u32[]{:S(2)}, u32[]{:S(2)}) collective-permute-start(bf16[4,8,2,32,128]{4,3,2,1,0:T(8,128)(2,1)} %scale_send.1), channel_id=1, source_target_pairs={{0,16},{16,0},{1,17},{17,1},{2,18},{18,2},{3,19},{19,3},{4,20},{20... | collective-permute-start | bytes 1572872 | tf_op jit(solution)/shard_map/ppermute | solution.py:137
  6.8 54.2 %copy-start = (f32[32768]{0:T(1024)S(1)}, f32[32768]{0:T(1024)}, u32[]{:S(2)}) copy-start(f32[32768]{0:T(1024)} %param.6) | copy-start | bytes 393220
  6.8 54.2 %copy-start.1 = (f32[32768]{0:T(1024)S(1)}, f32[32768]{0:T(1024)}, u32[]{:S(2)}) copy-start(f32[32768]{0:T(1024)} %param.7) | copy-start | bytes 393220
  6.8 54.2 %copy-start.2 = (f32[32768]{0:T(1024)S(1)}, f32[32768]{0:T(1024)}, u32[]{:S(2)}) copy-start(f32[32768]{0:T(1024)} %param.8) | copy-start | bytes 393220
  89.4 10.5 %collective-permute-start.1 = (bf16[4,17,32,128]{3,2,1,0:T(8,128)(2,1)S(1)}, bf16[4,17,32,128]{3,2,1,0:T(8,128)(2,1)S(1)}, u32[]{:S(2)}, u32[]{:S(2)}) collective-permute-start(bf16[4,17,32,128]{3,2,1,0:T(8,128)(2,1)S(1)} %all_to_all.29.refs_0_), channel_id=1, source_target_pairs={{0,16},{16,0},{1,17},{17,1},{2,18},{18,2},{3,19},{19,3},{4,20},{20... | collective-permute-start | bytes 1671176 | tf_op jit(solution)/shard_map/ppermute | solution.py:157

commit v8 on v6

--- a/solution.py
+++ b/solution.py
@@ -64,9 +64,8 @@
     for y in range(1, NY):
         total += parts[y].astype(f32)
     total = total.astype(bf16)
-    for z in range(NZL):
-        for zh in range(NZH):
-            out[z * NZH + zh] = total[zh]
+    for z in range(NZ):
+        out[z] = total[z // NZL]
 
 
 def update_kernel(parts, master, first, second, weights, grad):
@@ -151,7 +150,8 @@
     parts = jnp.sum(parts.astype(f32), axis=0).astype(bf16)
     parts = lax.all_to_all(parts, "y", 0, 0, tiled=True)
     parts = local(spread_kernel, jax.ShapeDtypeStruct((NZ, ROWS, 128), bf16), parts)
-    parts = lax.all_to_all(parts, ("zl", "zh"), 0, 0, tiled=True)
+    ring = [[(z % NZL) * NZH + z // NZL for z in range(NZ)]]
+    parts = lax.all_to_all(parts, ("zl", "zh"), 0, 0, tiled=True, axis_index_groups=ring)
     piece = jax.ShapeDtypeStruct((ROWS, 128), bf16)
     weights, grad = local(
         update_kernel, (jax.ShapeDtypeStruct((NS, ROWS, 128), bf16), piece), parts, master, first, second

time: 101 us -> 101 us (level)
  no operation moved by 1% of the time
where the time goes in v8:
time: 101 us
  blocking collectives  81.9 us (81%)
  starting transfers between devices  11.5 us (11%)
  Pallas kernels  5.58 us (6%)
    all_to_all x1, blocking collectives, shards(): lax.all_to_all(parts, ('zl', 'zh'), 0, 0, tiled=True, axis_index_groups=r...  26.5 us
    all_to_all x1, blocking collectives, shards(): lax.all_to_all(weights, ('zl', 'y', 'zh'), 0, 0, tiled=True, axis_index_g...  18.8 us
    all_to_all x1, blocking collectives, shards(): parts = lax.all_to_all(parts, 'y', 0, 0, tiled=True)  14.6 us
    all_to_all x1, blocking collectives, shards(): parts = lax.all_to_all(parts, 'x', 0, 0, tiled=True)  12.4 us
    all_to_all x1, blocking collectives, shards(): fan = lax.all_to_all(fan, 'x', 0, 0, tiled=True)  9.48 us
    ppermute x1, starting transfers between devices, shards(): other = lax.ppermute(fan, 'c', swap)  8.95 us
    pallas_call x2, Pallas kernels, scaled(): pl.pallas_call(functools.partial(scale_kernel, core), out_shape=jax.Shape...  3.47 us
    ppermute x1, starting transfers between devices, shards(): got = lax.ppermute(scaled(1), 'c', swap)  2.58 us
  transfers between devices with their start and end apart: 2, of which 2 were waited for; matrix products, arithmetic and copies ran while one was open for 0% of the time, Pallas kernels for 2%

profile of v8, /device:TPU:193, one launch (start us, length us, event | category | flops | bytes accessed | tf_op | source)
XLA Modules:
  0.0 100.7 jit_solution(6468908768976097063)
XLA Ops:
  0.6 0.0 copy-start.3
  0.6 2.1 %scale_send.1 = bf16[4,8,2,32,128]{4,3,2,1,0:T(8,128)(2,1)} custom-call(s32[64]{0:T(128)} %ranks.3, f32[8,2,2,128,128]{4,3,2,1,0:T(8,128)} %bitcast.17), custom_call_target="tpu_custom_call" | custom-call | flops 262144 | bytes 1572864 | tf_op jit(solution)/shard_map/scale_send/pallas_call | solution.py:119
  2.7 2.6 %collective-permute-start = (bf16[4,8,2,32,128]{4,3,2,1,0:T(8,128)(2,1)}, bf16[4,8,2,32,128]{4,3,2,1,0:T(8,128)(2,1)S(1)}, u32[]{:S(2)}, u32[]{:S(2)}) collective-permute-start(bf16[4,8,2,32,128]{4,3,2,1,0:T(8,128)(2,1)} %scale_send.1), channel_id=1, source_target_pairs={{0,16},{16,0},{1,17},{17,1},{2,18},{18,2},{3,19},{19,3},{4,20},{20... | collective-permute-start | bytes 1572872 | tf_op jit(solution)/shard_map/ppermute | solution.py:147
  5.3 0.0 copy-done.3
  5.3 1.4 %scale_own.1.own = bf16[4,8,2,32,128]{4,3,2,1,0:T(8,128)(2,1)S(1)} custom-call(s32[64]{0:T(128)S(1)} %copy-done.3, f32[8,2,2,128,128]{4,3,2,1,0:T(8,128)} %bitcast.18), custom_call_target="tpu_custom_call" | custom-call | flops 262144 | bytes 1572864 | tf_op jit(solution)/shard_map/scale_own/pallas_call | solution.py:119
  6.7 0.0 copy-start
  6.7 0.0 copy-start.1
  6.7 0.0 copy-start.2
  6.8 0.3 collective-permute-done.got
  7.0 0.1 combine_kernel.1
  7.2 12.4 %all_to_all.25 = bf16[4,8,2,32,128]{4,3,2,1,0:T(8,128)(2,1)S(1)} all-to-all(bf16[4,8,2,32,128]{4,3,2,1,0:T(8,128)(2,1)S(1)} %combine_kernel.1), channel_id=1, replica_groups=mesh['x'=4,'zl'=8,'c'=2,'y'=8,'zh'=2] {'x'}, dimensions={0} | all-to-all | bytes 1048576 | tf_op jit(solution)/shard_map/all_to_all | solution.py:149
  19.6 0.1 reduce_sum.12
  19.7 14.6 %all_to_all.26.parts = bf16[8,2,32,128]{3,2,1,0:T(8,128)(2,1)S(1)} all-to-all(bf16[8,2,32,128]{3,2,1,0:T(8,128)(2,1)S(1)} %reduce_sum.12), channel_id=1, replica_groups=mesh['x'=4,'zl'=8,'c'=2,'y'=8,'zh'=2] {'y'}, dimensions={0} | all-to-all | bytes 262144 | tf_op jit(solution)/shard_map/all_to_all | solution.py:151
  34.4 26.5 %all_to_all.27.parts = bf16[16,32,128]{2,1,0:T(8,128)(2,1)S(1)} all-to-all(bf16[16,32,128]{2,1,0:T(8,128)(2,1)S(1)} %spread_kernel.1), channel_id=1, replica_groups={{0,32,64,96,128,160,192,224,1,33,65,97,129,161,193,225},{2,34,66,98,130..., dimensions={0} | all-to-all | bytes 262144 | tf_op jit(solution)/shard_map/all_to_all | solution.py:154
  60.9 0.0 copy-done
  60.9 0.0 copy-done.1
  60.9 0.0 copy-done.2
  60.9 0.1 update_kernel.1
  61.0 18.8 %all_to_all.28.weights = bf16[16,32,128]{2,1,0:T(8,128)(2,1)S(1)} all-to-all(bf16[16,32,128]{2,1,0:T(8,128)(2,1)S(1)} %get-tuple-element.14), channel_id=1, replica_groups={{0,225,2,227,4,229,6,231,8,233,10,235,12,237,14,239},{32,193,34,195,36,..., dimensions={0} | all-to-all | bytes 262144 | tf_op jit(solution)/shard_map/all_to_all | solution.py:163
  79.7 0.1 fan_kernel.1
  79.8 9.5 %all_to_all.29.refs_0_ = bf16[4,17,32,128]{3,2,1,0:T(8,128)(2,1)S(1)} all-to-all(bf16[4,17,32,128]{3,2,1,0:T(8,128)(2,1)S(1)} %fan_kernel.1), channel_id=1, replica_groups=mesh['x'=4,'zl'=8,'c'=2,'y'=8,'zh'=2] {'x'}, dimensions={0} | all-to-all | bytes 1114112 | tf_op jit(solution)/shard_map/all_to_all | solution.py:165
  89.3 8.9 %collective-permute-start.1 = (bf16[4,17,32,128]{3,2,1,0:T(8,128)(2,1)S(1)}, bf16[4,17,32,128]{3,2,1,0:T(8,128)(2,1)S(1)}, u32[]{:S(2)}, u32[]{:S(2)}) collective-permute-start(bf16[4,17,32,128]{3,2,1,0:T(8,128)(2,1)S(1)} %all_to_all.29.refs_0_), channel_id=1, source_target_pairs={{0,16},{16,0},{1,17},{17,1},{2,18},{18,2},{3,19},{19,3},{4,20},{20... | collective-permute-start | bytes 1671176 | tf_op jit(solution)/shard_map/ppermute | solution.py:166
  98.3 0.9 finish_own.1
  99.2 0.6 collective-permute-done.1.refs_0_
  99.8 0.9 finish_partner.1
  (1 shorter events, 0.0 us)
Async XLA Ops:
  0.6 4.7 %copy-start.3 = (s32[64]{0:T(128)S(1)}, s32[64]{0:T(128)}, u32[]{:S(2)}) copy-start(s32[64]{0:T(128)} %ranks.3) | copy-start | bytes 772
  2.7 4.3 %collective-permute-start = (bf16[4,8,2,32,128]{4,3,2,1,0:T(8,128)(2,1)}, bf16[4,8,2,32,128]{4,3,2,1,0:T(8,128)(2,1)S(1)}, u32[]{:S(2)}, u32[]{:S(2)}) collective-permute-start(bf16[4,8,2,32,128]{4,3,2,1,0:T(8,128)(2,1)} %scale_send.1), channel_id=1, source_target_pairs={{0,16},{16,0},{1,17},{17,1},{2,18},{18,2},{3,19},{19,3},{4,20},{20... | collective-permute-start | bytes 1572872 | tf_op jit(solution)/shard_map/ppermute | solution.py:147
  6.7 54.2 %copy-start = (f32[32768]{0:T(1024)S(1)}, f32[32768]{0:T(1024)}, u32[]{:S(2)}) copy-start(f32[32768]{0:T(1024)} %param.6) | copy-start | bytes 393220
  6.7 54.2 %copy-start.1 = (f32[32768]{0:T(1024)S(1)}, f32[32768]{0:T(1024)}, u32[]{:S(2)}) copy-start(f32[32768]{0:T(1024)} %param.7) | copy-start | bytes 393220
  6.7 54.2 %copy-start.2 = (f32[32768]{0:T(1024)S(1)}, f32[32768]{0:T(1024)}, u32[]{:S(2)}) copy-start(f32[32768]{0:T(1024)} %param.8) | copy-start | bytes 393220
  89.3 10.5 %collective-permute-start.1 = (bf16[4,17,32,128]{3,2,1,0:T(8,128)(2,1)S(1)}, bf16[4,17,32,128]{3,2,1,0:T(8,128)(2,1)S(1)}, u32[]{:S(2)}, u32[]{:S(2)}) collective-permute-start(bf16[4,17,32,128]{3,2,1,0:T(8,128)(2,1)S(1)} %all_to_all.29.refs_0_), channel_id=1, source_target_pairs={{0,16},{16,0},{1,17},{17,1},{2,18},{18,2},{3,19},{19,3},{4,20},{20... | collective-permute-start | bytes 1671176 | tf_op jit(solution)/shard_map/ppermute | solution.py:166
